TPU v7x, 32 devices: a whole 2x2x4 slice. The times are simulated.
32 devices in a mesh: ty: 4 (over y, core), tx: 8 (over z, x).
Axes of the slice: x: 2, y: 2, z: 4, core: 2. Of those that a mesh axis runs over, the one named last changes fastest.
Arguments:
- object_field: bfloat16 [2, 1024, 2048], P(None, 'ty', 'tx'), may hold values from -5 to 5
- probe_field: float32 [2, 256, 256], replicated, may hold values from -2.1 to 2.1
- corners: int32 [4, 8, 8, 2], P('ty', 'tx'), may hold values from 0 to 255, as said below
- counts: int32 [4, 8], P('ty', 'tx'), may hold values from 0 to 8, as said below
- intensity: bfloat16 [4, 8, 8, 256, 256], P('ty', 'tx'), may hold values from 0 to 1.5
- damping: float32 [], replicated, may hold values from 0.5 to 4
Outputs:
- update: float32 [2, 1024, 2048], P(None, 'ty', 'tx')
Inputs may be any that keep to these rules, and one draw needn't show every extreme that they name: `corners`: A patch lies inside the object: on the last tile row (column) of devices the corner's row (column) is 0. A device's live slots are its first counts slots. The counts of the devices of one column (same tx index) sum to exactly 16, and some device of every column holds 8.
All inputs are finite; a program needn't handle non-finite values.
Results may differ from a plain program's by a relative error of at most 0.015.
Values may be sent and summed in bfloat16 or wider, within the bound.
A program may use at most 64 MiB of HBM per device.

v0:
```python
import jax
import jax.numpy as jnp
from jax import lax
from jax.sharding import PartitionSpec as P


def from_behind(block, axis, distance):
    devices = range(lax.axis_size(axis))
    route = [(i - distance, i) for i in devices if i - distance in devices]
    return lax.ppermute(block, axis, route)


def make_table(extent, direction_sign):
    indices = jnp.arange(extent, dtype=jnp.int32)
    phases = (indices[:, None] * indices[None, :] % extent).astype(jnp.float32)
    angles = phases * (2.0 * jnp.pi / extent)
    norm_scale = 1.0 / float(extent) ** 0.5
    cosine = jnp.cos(angles) * norm_scale
    sines = direction_sign * jnp.sin(angles) * norm_scale
    tables = jnp.stack([jnp.stack([cosine, sines], 1), jnp.stack([-sines, cosine], 1)], 0)
    return tables.astype(jnp.bfloat16)


def transform(field, tables):
    halfway = jnp.einsum(
        "btrc,tcsk->bsrk", field, tables, preferred_element_type=jnp.float32
    ).astype(jnp.bfloat16)
    return jnp.einsum("btrc,trsk->bskc", halfway, tables, preferred_element_type=jnp.float32)


def times_probe(probe_field, patches):
    real_part = probe_field[0] * patches[:, 0] - probe_field[1] * patches[:, 1]
    imag_part = probe_field[0] * patches[:, 1] + probe_field[1] * patches[:, 0]
    return jnp.stack([real_part, imag_part], 1)


def times_conj_probe(probe_field, returned):
    real_part = probe_field[0] * returned[:, 0] + probe_field[1] * returned[:, 1]
    imag_part = probe_field[0] * returned[:, 1] - probe_field[1] * returned[:, 0]
    return jnp.stack([real_part, imag_part], 1)


def residual_waves(exit_wave, measured, forward, inverse):
    far_field = transform(exit_wave, forward)
    powers = far_field[:, 0] * far_field[:, 0] + far_field[:, 1] * far_field[:, 1]
    misfit = powers - measured.astype(jnp.float32)
    returned = transform((far_field * misfit[:, None]).astype(jnp.bfloat16), inverse).astype(
        jnp.bfloat16
    )
    return (far_field, returned)


def product_waves(exit_wave, far_field, forward, inverse):
    image_field = transform(exit_wave, forward)
    projected = far_field[:, 0] * image_field[:, 0] + far_field[:, 1] * image_field[:, 1]
    return transform((far_field * projected[:, None]).astype(jnp.bfloat16), inverse).astype(
        jnp.bfloat16
    )


def fetch_margins(field):
    from_right = from_behind(field, "tx", -1)
    widened = jnp.concatenate([field, from_right], 2)
    from_below = from_behind(widened, "ty", -1)
    return jnp.concatenate([widened, from_below], 1)


def accumulate(contribs, places, tile_len, extent):
    extended = jnp.zeros((2, tile_len + extent, tile_len + extent), jnp.float32)

    def add_patch(k, running):
        anchor = jnp.zeros((), jnp.int32)
        previous = lax.dynamic_slice(
            running, (anchor, places[k, 0], places[k, 1]), (2, extent, extent)
        )
        return lax.dynamic_update_slice(
            running, previous + contribs[k], (anchor, places[k, 0], places[k, 1])
        )

    return lax.fori_loop(0, contribs.shape[0], add_patch, extended)


def fold_margins(extended, tile_len):
    extent = extended.shape[1] - tile_len
    arrived = from_behind(extended[:, :, tile_len:], "tx", 1)
    inner_part = extended[:, :, :tile_len].at[:, :, :extent].add(arrived)
    arrived_rows = from_behind(inner_part[:, tile_len:, :], "ty", 1)
    return inner_part[:, :tile_len, :].at[:, :extent, :].add(arrived_rows)


def per_device(object_field, probe_field, corners, counts, intensity, damping):
    extent = probe_field.shape[-1]
    tile_len = object_field.shape[1]
    slot_count = corners.shape[2]
    places = corners.reshape(slot_count, 2)
    own_count = counts.reshape(())
    alive_mask = (jnp.arange(slot_count, dtype=jnp.int32) < own_count).astype(jnp.float32)
    measured = intensity.reshape(slot_count, extent, extent)
    forward = make_table(extent, -1.0)
    inverse = make_table(extent, 1.0)

    def waves_from(field):
        widened = fetch_margins(field)
        anchor = jnp.zeros((), jnp.int32)
        patches = jax.vmap(
            lambda r, c: lax.dynamic_slice(widened, (anchor, r, c), (2, extent, extent))
        )(places[:, 0], places[:, 1])
        return times_probe(probe_field, patches.astype(jnp.float32)).astype(jnp.bfloat16)

    def collect_terms(returned, weight_factor):
        contribs = weight_factor * times_conj_probe(probe_field, returned.astype(jnp.float32))
        contribs = contribs * alive_mask[:, None, None, None]
        return fold_margins(accumulate(contribs, places, tile_len, extent), tile_len)

    def product_pass(exit_wave, far_field):
        return product_waves(exit_wave, far_field, forward, inverse)

    far_field, returned = residual_waves(waves_from(object_field), measured, forward, inverse)

    def apply_system(direction):
        moved = product_pass(waves_from(direction.astype(jnp.bfloat16)), far_field)
        return collect_terms(moved, 4.0) + damping * direction

    residual = -collect_terms(returned, 2.0)
    direction = residual
    norm_now = lax.psum(jnp.sum(residual * residual), ("ty", "tx"))
    image_field = apply_system(direction)
    curvature, image_square = lax.psum(
        (jnp.sum(direction * image_field), jnp.sum(image_field * image_field)), ("ty", "tx")
    )
    step_len = norm_now / curvature
    norm_next = norm_now - 2.0 * step_len * curvature + step_len * step_len * image_square
    residual = residual - step_len * image_field
    solution = step_len * direction
    direction = residual + norm_next / norm_now * direction
    image_field = apply_system(direction)
    step_len = norm_next / lax.psum(jnp.sum(direction * image_field), ("ty", "tx"))
    return solution + step_len * direction


def solution(mesh):
    in_specs = (
        P(None, "ty", "tx"),
        P(),
        P("ty", "tx", None, None),
        P("ty", "tx"),
        P("ty", "tx", None, None, None),
        P(),
    )
    out_specs = P(None, "ty", "tx")
    return jax.shard_map(
        per_device, mesh=mesh, in_specs=in_specs, out_specs=out_specs, check_vma=False
    )
```

profile of v0, /device:TPU:0, one launch (start us, length us, event | category | flops | bytes accessed | tf_op | source)
XLA Modules:
  0.0 756.5 jit_solution(18385443316733693185)
XLA Ops:
  6.8 4.5 collective-permute-done
  16.4 24.8 %while.57 = (s32[]{:T(128)}, bf16[2,512,512]{2,1,0:T(8,128)(2,1)}, s32[8,3]{0,1:T(4,128)S(1)}, bf16[8,2,256,256]{3,2,0,1:T(8,128)(2,1)S(1)}, s32[]{:T(128)}) while((s32[]{:T(128)}, bf16[2,512,512]{2,1,0:T(8,128)(2,1)}, s32[8,3]{0,1:T(4,128)S(1)}, bf16[8,2,256,256]{3,2,0,1:T(8,128)(2,1)S(1)}, s32[]{:T(128)}) %tuple.188), condition=%wide.while_cond.6, body=%wide.while_body.6.sunk | while | flops 2 | bytes 524405 | solution.py:106
  17.1 2.5 bitcast_dynamic-update-slice_fusion.6
  20.1 2.5 bitcast_dynamic-update-slice_fusion.6
  23.2 2.5 bitcast_dynamic-update-slice_fusion.6
  26.3 2.5 bitcast_dynamic-update-slice_fusion.6
  42.3 5.4 convolution_bitcast_fusion.2
  47.6 2.9 fusion.15
  50.5 6.6 convert_bitcast_fusion.2
  57.1 2.8 multiply_add_fusion.2
  59.9 2.6 maximum_multiply_fusion
  63.1 114.6 %while.54 = (s32[]{:T(128)}, f32[2,512,512]{2,1,0:T(8,128)S(1)}, s32[8,2]{0,1:T(2,128)S(1)}, f32[8,2,256,256]{3,2,0,1:T(8,128)}, s32[]{:T(128)}, /*index=5*/s32[]{:T(128)}, s32[]{:T(128)}) while((s32[]{:T(128)}, f32[2,512,512]{2,1,0:T(8,128)S(1)}, s32[8,2]{0,1:T(2,128)S(1)}, f32[8,2,256,256]{3,2,0,1:T(8,128)}, s32[]{:T(128)}, ...), condition=%wide.region_1.2_spmd, body=%wide.region_0.1_spmd.sunk | while | flops 131080 | bytes 2621621 | solution.py:80
  68.6 8.9 %dynamic_update_slice.24 = f32[2,512,512]{2,1,0:T(8,128)S(1)} dynamic-update-slice(f32[2,512,512]{2,1,0:T(8,128)S(1)} %get-tuple-element.693, f32[2,256,256]{2,1,0:T(8,128)S(1)} %bitcast_add_fusion.6, s32[]{:T(128)} %constant.304.clone.1..sunk, s32[]{:T(128)S(6)} %select_n.161, s32[]{:T(128)S(6)} %select_n.162) | dynamic-update-slice | bytes 1048580 | tf_op jit(solution)/shard_map/while/body/eval_jaxpr/dynamic_update_slice | solution.py:76
  83.0 7.4 dynamic_update_slice.24
  95.9 9.4 %dynamic_update_slice.24 = f32[2,512,512]{2,1,0:T(8,128)S(1)} dynamic-update-slice(f32[2,512,512]{2,1,0:T(8,128)S(1)} %get-tuple-element.693, f32[2,256,256]{2,1,0:T(8,128)S(1)} %bitcast_add_fusion.6, s32[]{:T(128)} %constant.304.clone.1..sunk, s32[]{:T(128)S(6)} %select_n.161, s32[]{:T(128)S(6)} %select_n.162) | dynamic-update-slice | bytes 1048580 | tf_op jit(solution)/shard_map/while/body/eval_jaxpr/dynamic_update_slice | solution.py:76
  110.8 8.3 %dynamic_update_slice.24 = f32[2,512,512]{2,1,0:T(8,128)S(1)} dynamic-update-slice(f32[2,512,512]{2,1,0:T(8,128)S(1)} %get-tuple-element.693, f32[2,256,256]{2,1,0:T(8,128)S(1)} %bitcast_add_fusion.6, s32[]{:T(128)} %constant.304.clone.1..sunk, s32[]{:T(128)S(6)} %select_n.161, s32[]{:T(128)S(6)} %select_n.162) | dynamic-update-slice | bytes 1048580 | tf_op jit(solution)/shard_map/while/body/eval_jaxpr/dynamic_update_slice | solution.py:76
  124.7 9.0 %dynamic_update_slice.24 = f32[2,512,512]{2,1,0:T(8,128)S(1)} dynamic-update-slice(f32[2,512,512]{2,1,0:T(8,128)S(1)} %get-tuple-element.693, f32[2,256,256]{2,1,0:T(8,128)S(1)} %bitcast_add_fusion.6, s32[]{:T(128)} %constant.304.clone.1..sunk, s32[]{:T(128)S(6)} %select_n.161, s32[]{:T(128)S(6)} %select_n.162) | dynamic-update-slice | bytes 1048580 | tf_op jit(solution)/shard_map/while/body/eval_jaxpr/dynamic_update_slice | solution.py:76
  139.2 10.8 %dynamic_update_slice.24 = f32[2,512,512]{2,1,0:T(8,128)S(1)} dynamic-update-slice(f32[2,512,512]{2,1,0:T(8,128)S(1)} %get-tuple-element.693, f32[2,256,256]{2,1,0:T(8,128)S(1)} %bitcast_add_fusion.6, s32[]{:T(128)} %constant.304.clone.1..sunk, s32[]{:T(128)S(6)} %select_n.161, s32[]{:T(128)S(6)} %select_n.162) | dynamic-update-slice | bytes 1048580 | tf_op jit(solution)/shard_map/while/body/eval_jaxpr/dynamic_update_slice | solution.py:76
  155.6 9.0 %dynamic_update_slice.24 = f32[2,512,512]{2,1,0:T(8,128)S(1)} dynamic-update-slice(f32[2,512,512]{2,1,0:T(8,128)S(1)} %get-tuple-element.693, f32[2,256,256]{2,1,0:T(8,128)S(1)} %bitcast_add_fusion.6, s32[]{:T(128)} %constant.304.clone.1..sunk, s32[]{:T(128)S(6)} %select_n.161, s32[]{:T(128)S(6)} %select_n.162) | dynamic-update-slice | bytes 1048580 | tf_op jit(solution)/shard_map/while/body/eval_jaxpr/dynamic_update_slice | solution.py:76
  170.1 7.7 %dynamic_update_slice.24 = f32[2,512,512]{2,1,0:T(8,128)S(1)} dynamic-update-slice(f32[2,512,512]{2,1,0:T(8,128)S(1)} %get-tuple-element.693, f32[2,256,256]{2,1,0:T(8,128)S(1)} %bitcast_add_fusion.6, s32[]{:T(128)} %constant.304.clone.1..sunk, s32[]{:T(128)S(6)} %select_n.161, s32[]{:T(128)S(6)} %select_n.162) | dynamic-update-slice | bytes 1048580 | tf_op jit(solution)/shard_map/while/body/eval_jaxpr/dynamic_update_slice | solution.py:76
  177.9 6.1 collective-permute-start.2
  183.9 21.3 %collective-permute-done.2 = f32[2,512,256]{2,1,0:T(8,128)S(1)} collective-permute-done((f32[2,512,256]{2,1,0:T(8,128)S(1)}, f32[2,512,256]{2,1,0:T(8,128)S(1)}, u32[]{:S(2)}, u32[]{:S(2)}) %collective-permute-start.2) | collective-permute-done | bytes 1048608 | tf_op jit(solution)/shard_map/ppermute | solution.py:10
  205.5 4.2 collective-permute-start.3
  212.6 7.1 collective-permute-done.4
  221.2 8.0 %collective-permute-done.5 = bf16[2,256,512]{2,1,0:T(8,128)(2,1)S(1)} collective-permute-done((bf16[2,256,512]{2,1,0:T(8,128)(2,1)S(1)}, bf16[2,256,512]{2,1,0:T(8,128)(2,1)S(1)}, u32[]{:S(2)}, u32[]{:S(2)}) %collective-permute-start.5) | collective-permute-done | bytes 524320 | tf_op jit(solution)/shard_map/ppermute | solution.py:10
  230.5 24.8 %while.58 = (s32[]{:T(128)}, bf16[2,512,512]{2,1,0:T(8,128)(2,1)}, s32[8,3]{0,1:T(4,128)S(1)}, bf16[8,2,256,256]{3,2,0,1:T(8,128)(2,1)S(1)}, s32[]{:T(128)}) while((s32[]{:T(128)}, bf16[2,512,512]{2,1,0:T(8,128)(2,1)}, s32[8,3]{0,1:T(4,128)S(1)}, bf16[8,2,256,256]{3,2,0,1:T(8,128)(2,1)S(1)}, s32[]{:T(128)}) %tuple.206), condition=%wide.while_cond.7, body=%wide.while_body.7.sunk | while | flops 2 | bytes 524405 | solution.py:106
  256.9 5.4 convolution_bitcast_fusion.1
  262.3 4.1 fusion.6
  266.4 6.9 convert_bitcast_fusion.1
  273.3 2.8 multiply_add_fusion.1
  276.1 2.6 maximum_multiply_fusion.1
  278.9 114.7 %while.55 = (s32[]{:T(128)}, f32[2,512,512]{2,1,0:T(8,128)S(1)}, s32[8,2]{0,1:T(2,128)S(1)}, f32[8,2,256,256]{3,2,0,1:T(8,128)}, s32[]{:T(128)}, /*index=5*/s32[]{:T(128)}, s32[]{:T(128)}) while((s32[]{:T(128)}, f32[2,512,512]{2,1,0:T(8,128)S(1)}, s32[8,2]{0,1:T(2,128)S(1)}, f32[8,2,256,256]{3,2,0,1:T(8,128)}, s32[]{:T(128)}, ...), condition=%wide.region_5.6_spmd, body=%wide.region_4.5_spmd.sunk | while | flops 131080 | bytes 2621621 | solution.py:80
  284.4 8.9 %dynamic_update_slice.25 = f32[2,512,512]{2,1,0:T(8,128)S(1)} dynamic-update-slice(f32[2,512,512]{2,1,0:T(8,128)S(1)} %get-tuple-element.729, f32[2,256,256]{2,1,0:T(8,128)S(1)} %bitcast_add_fusion.7, s32[]{:T(128)} %constant.304.clone.1..sunk.1, s32[]{:T(128)S(6)} %select_n.163, s32[]{:T(128)S(6)} %select_n.164) | dynamic-update-slice | bytes 1048580 | tf_op jit(solution)/shard_map/while/body/eval_jaxpr/dynamic_update_slice | solution.py:76
  298.8 7.4 dynamic_update_slice.25
  311.7 9.4 %dynamic_update_slice.25 = f32[2,512,512]{2,1,0:T(8,128)S(1)} dynamic-update-slice(f32[2,512,512]{2,1,0:T(8,128)S(1)} %get-tuple-element.729, f32[2,256,256]{2,1,0:T(8,128)S(1)} %bitcast_add_fusion.7, s32[]{:T(128)} %constant.304.clone.1..sunk.1, s32[]{:T(128)S(6)} %select_n.163, s32[]{:T(128)S(6)} %select_n.164) | dynamic-update-slice | bytes 1048580 | tf_op jit(solution)/shard_map/while/body/eval_jaxpr/dynamic_update_slice | solution.py:76
  326.7 8.3 %dynamic_update_slice.25 = f32[2,512,512]{2,1,0:T(8,128)S(1)} dynamic-update-slice(f32[2,512,512]{2,1,0:T(8,128)S(1)} %get-tuple-element.729, f32[2,256,256]{2,1,0:T(8,128)S(1)} %bitcast_add_fusion.7, s32[]{:T(128)} %constant.304.clone.1..sunk.1, s32[]{:T(128)S(6)} %select_n.163, s32[]{:T(128)S(6)} %select_n.164) | dynamic-update-slice | bytes 1048580 | tf_op jit(solution)/shard_map/while/body/eval_jaxpr/dynamic_update_slice | solution.py:76
  340.5 9.0 %dynamic_update_slice.25 = f32[2,512,512]{2,1,0:T(8,128)S(1)} dynamic-update-slice(f32[2,512,512]{2,1,0:T(8,128)S(1)} %get-tuple-element.729, f32[2,256,256]{2,1,0:T(8,128)S(1)} %bitcast_add_fusion.7, s32[]{:T(128)} %constant.304.clone.1..sunk.1, s32[]{:T(128)S(6)} %select_n.163, s32[]{:T(128)S(6)} %select_n.164) | dynamic-update-slice | bytes 1048580 | tf_op jit(solution)/shard_map/while/body/eval_jaxpr/dynamic_update_slice | solution.py:76
  355.1 10.8 %dynamic_update_slice.25 = f32[2,512,512]{2,1,0:T(8,128)S(1)} dynamic-update-slice(f32[2,512,512]{2,1,0:T(8,128)S(1)} %get-tuple-element.729, f32[2,256,256]{2,1,0:T(8,128)S(1)} %bitcast_add_fusion.7, s32[]{:T(128)} %constant.304.clone.1..sunk.1, s32[]{:T(128)S(6)} %select_n.163, s32[]{:T(128)S(6)} %select_n.164) | dynamic-update-slice | bytes 1048580 | tf_op jit(solution)/shard_map/while/body/eval_jaxpr/dynamic_update_slice | solution.py:76
  371.4 9.0 %dynamic_update_slice.25 = f32[2,512,512]{2,1,0:T(8,128)S(1)} dynamic-update-slice(f32[2,512,512]{2,1,0:T(8,128)S(1)} %get-tuple-element.729, f32[2,256,256]{2,1,0:T(8,128)S(1)} %bitcast_add_fusion.7, s32[]{:T(128)} %constant.304.clone.1..sunk.1, s32[]{:T(128)S(6)} %select_n.163, s32[]{:T(128)S(6)} %select_n.164) | dynamic-update-slice | bytes 1048580 | tf_op jit(solution)/shard_map/while/body/eval_jaxpr/dynamic_update_slice | solution.py:76
  385.9 7.7 %dynamic_update_slice.25 = f32[2,512,512]{2,1,0:T(8,128)S(1)} dynamic-update-slice(f32[2,512,512]{2,1,0:T(8,128)S(1)} %get-tuple-element.729, f32[2,256,256]{2,1,0:T(8,128)S(1)} %bitcast_add_fusion.7, s32[]{:T(128)} %constant.304.clone.1..sunk.1, s32[]{:T(128)S(6)} %select_n.163, s32[]{:T(128)S(6)} %select_n.164) | dynamic-update-slice | bytes 1048580 | tf_op jit(solution)/shard_map/while/body/eval_jaxpr/dynamic_update_slice | solution.py:76
  393.7 6.1 collective-permute-start.6
  399.8 18.8 %collective-permute-done.6 = f32[2,512,256]{2,1,0:T(8,128)S(1)} collective-permute-done((f32[2,512,256]{2,1,0:T(8,128)S(1)}, f32[2,512,256]{2,1,0:T(8,128)S(1)}, u32[]{:S(2)}, u32[]{:S(2)}) %collective-permute-start.6) | collective-permute-done | bytes 1048608 | tf_op jit(solution)/shard_map/ppermute | solution.py:10
  419.8 6.7 collective-permute-start.7
  429.9 56.1 %all-reduce = (f32[]{:T(128)}, f32[]{:T(128)}, f32[]{:T(128)}) all-reduce(f32[]{:T(128)} %get-tuple-element.403, f32[]{:T(128)} %get-tuple-element.402, f32[]{:T(128)} %get-tuple-element.401), channel_id=1, replica_groups=mesh['ty'=4,'tx'=8] {'ty','tx'}, use_global_device_ids=true, to_apply=%region_3.4 | all-reduce | flops 3 | bytes 24 | tf_op jit(solution)/shard_map/psum | solution.py:126
  491.3 9.1 %collective-permute-done.8 = bf16[2,256,256]{2,1,0:T(8,128)(2,1)S(1)} collective-permute-done((bf16[2,256,256]{2,1,0:T(8,128)(2,1)S(1)}, bf16[2,256,256]{2,1,0:T(8,128)(2,1)S(1)}, u32[]{:S(2)}, u32[]{:S(2)}) %collective-permute-start.8) | collective-permute-done | bytes 262176 | tf_op jit(solution)/shard_map/ppermute | solution.py:10
  505.6 24.4 %while.59 = (s32[]{:T(128)}, bf16[2,512,512]{2,1,0:T(8,128)(2,1)}, s32[8,3]{0,1:T(4,128)S(1)}, bf16[8,2,256,256]{3,2,0,1:T(8,128)(2,1)S(1)}, s32[]{:T(128)}) while((s32[]{:T(128)}, bf16[2,512,512]{2,1,0:T(8,128)(2,1)}, s32[8,3]{0,1:T(4,128)S(1)}, bf16[8,2,256,256]{3,2,0,1:T(8,128)(2,1)S(1)}, s32[]{:T(128)}) %tuple.207), condition=%wide.while_cond.8, body=%wide.while_body.8.sunk | while | flops 2 | bytes 524405 | solution.py:106
  531.9 5.4 convolution_bitcast_fusion
  537.3 4.1 fusion.4
  541.4 6.9 convert_bitcast_fusion
  548.3 2.8 multiply_add_fusion
  551.1 2.5 maximum_multiply_fusion.2
  553.8 117.9 %while.56 = (s32[]{:T(128)}, f32[2,512,512]{2,1,0:T(8,128)S(1)}, s32[8,2]{0,1:T(2,128)S(1)}, f32[8,2,256,256]{3,2,0,1:T(8,128)}, s32[]{:T(128)}, /*index=5*/s32[]{:T(128)}, s32[]{:T(128)}) while((s32[]{:T(128)}, f32[2,512,512]{2,1,0:T(8,128)S(1)}, s32[8,2]{0,1:T(2,128)S(1)}, f32[8,2,256,256]{3,2,0,1:T(8,128)}, s32[]{:T(128)}, ...), condition=%wide.region_11.12_spmd, body=%wide.region_10.11_spmd.sunk | while | flops 131080 | bytes 2621621 | solution.py:80
  559.7 8.9 %dynamic_update_slice.26 = f32[2,512,512]{2,1,0:T(8,128)S(1)} dynamic-update-slice(f32[2,512,512]{2,1,0:T(8,128)S(1)} %get-tuple-element.765, f32[2,256,256]{2,1,0:T(8,128)S(1)} %bitcast_add_fusion.8, s32[]{:T(128)} %constant.304.clone.1..sunk.2, s32[]{:T(128)S(6)} %select_n.165, s32[]{:T(128)S(6)} %select_n.166) | dynamic-update-slice | bytes 1048580 | tf_op jit(solution)/shard_map/while/body/eval_jaxpr/dynamic_update_slice | solution.py:76
  574.6 7.4 dynamic_update_slice.26
  587.9 9.4 %dynamic_update_slice.26 = f32[2,512,512]{2,1,0:T(8,128)S(1)} dynamic-update-slice(f32[2,512,512]{2,1,0:T(8,128)S(1)} %get-tuple-element.765, f32[2,256,256]{2,1,0:T(8,128)S(1)} %bitcast_add_fusion.8, s32[]{:T(128)} %constant.304.clone.1..sunk.2, s32[]{:T(128)S(6)} %select_n.165, s32[]{:T(128)S(6)} %select_n.166) | dynamic-update-slice | bytes 1048580 | tf_op jit(solution)/shard_map/while/body/eval_jaxpr/dynamic_update_slice | solution.py:76
  603.2 8.3 %dynamic_update_slice.26 = f32[2,512,512]{2,1,0:T(8,128)S(1)} dynamic-update-slice(f32[2,512,512]{2,1,0:T(8,128)S(1)} %get-tuple-element.765, f32[2,256,256]{2,1,0:T(8,128)S(1)} %bitcast_add_fusion.8, s32[]{:T(128)} %constant.304.clone.1..sunk.2, s32[]{:T(128)S(6)} %select_n.165, s32[]{:T(128)S(6)} %select_n.166) | dynamic-update-slice | bytes 1048580 | tf_op jit(solution)/shard_map/while/body/eval_jaxpr/dynamic_update_slice | solution.py:76
  617.4 9.0 %dynamic_update_slice.26 = f32[2,512,512]{2,1,0:T(8,128)S(1)} dynamic-update-slice(f32[2,512,512]{2,1,0:T(8,128)S(1)} %get-tuple-element.765, f32[2,256,256]{2,1,0:T(8,128)S(1)} %bitcast_add_fusion.8, s32[]{:T(128)} %constant.304.clone.1..sunk.2, s32[]{:T(128)S(6)} %select_n.165, s32[]{:T(128)S(6)} %select_n.166) | dynamic-update-slice | bytes 1048580 | tf_op jit(solution)/shard_map/while/body/eval_jaxpr/dynamic_update_slice | solution.py:76
  632.4 10.8 %dynamic_update_slice.26 = f32[2,512,512]{2,1,0:T(8,128)S(1)} dynamic-update-slice(f32[2,512,512]{2,1,0:T(8,128)S(1)} %get-tuple-element.765, f32[2,256,256]{2,1,0:T(8,128)S(1)} %bitcast_add_fusion.8, s32[]{:T(128)} %constant.304.clone.1..sunk.2, s32[]{:T(128)S(6)} %select_n.165, s32[]{:T(128)S(6)} %select_n.166) | dynamic-update-slice | bytes 1048580 | tf_op jit(solution)/shard_map/while/body/eval_jaxpr/dynamic_update_slice | solution.py:76
  649.1 9.0 %dynamic_update_slice.26 = f32[2,512,512]{2,1,0:T(8,128)S(1)} dynamic-update-slice(f32[2,512,512]{2,1,0:T(8,128)S(1)} %get-tuple-element.765, f32[2,256,256]{2,1,0:T(8,128)S(1)} %bitcast_add_fusion.8, s32[]{:T(128)} %constant.304.clone.1..sunk.2, s32[]{:T(128)S(6)} %select_n.165, s32[]{:T(128)S(6)} %select_n.166) | dynamic-update-slice | bytes 1048580 | tf_op jit(solution)/shard_map/while/body/eval_jaxpr/dynamic_update_slice | solution.py:76
  664.0 7.7 %dynamic_update_slice.26 = f32[2,512,512]{2,1,0:T(8,128)S(1)} dynamic-update-slice(f32[2,512,512]{2,1,0:T(8,128)S(1)} %get-tuple-element.765, f32[2,256,256]{2,1,0:T(8,128)S(1)} %bitcast_add_fusion.8, s32[]{:T(128)} %constant.304.clone.1..sunk.2, s32[]{:T(128)S(6)} %select_n.165, s32[]{:T(128)S(6)} %select_n.166) | dynamic-update-slice | bytes 1048580 | tf_op jit(solution)/shard_map/while/body/eval_jaxpr/dynamic_update_slice | solution.py:76
  671.8 6.2 collective-permute-start.10
  678.0 22.2 %collective-permute-done.10 = f32[2,512,256]{2,1,0:T(8,128)S(1)} collective-permute-done((f32[2,512,256]{2,1,0:T(8,128)S(1)}, f32[2,512,256]{2,1,0:T(8,128)S(1)}, u32[]{:S(2)}, u32[]{:S(2)}) %collective-permute-start.10) | collective-permute-done | bytes 1048608 | tf_op jit(solution)/shard_map/ppermute | solution.py:10
  700.5 3.3 collective-permute-start.11
  706.1 48.9 %psum.31 = f32[]{:T(128)} all-reduce(f32[]{:T(128)} %fusion.55), channel_id=1, replica_groups=mesh['ty'=4,'tx'=8] {'ty','tx'}, use_global_device_ids=true, to_apply=%region_13.14 | all-reduce | flops 1 | bytes 8 | tf_op jit(solution)/shard_map/psum | solution.py:137
  (192 shorter events, 145.8 us)
Async XLA Ops:
  0.0 11.3 %collective-permute-start = (bf16[2,256,256]{2,1,0:T(8,128)(2,1)}, bf16[2,256,256]{2,1,0:T(8,128)(2,1)S(1)}, u32[]{:S(2)}, u32[]{:S(2)}) collective-permute-start(bf16[2,256,256]{2,1,0:T(8,128)(2,1)} %param.36), channel_id=1, source_target_pairs={{1,0},{2,1},{3,2},{4,3},{5,4},{6,5},{7,6},{9,8},{10,9},{11,10},{12... | collective-permute-start | bytes 786440 | tf_op jit(solution)/shard_map/ppermute | solution.py:10
  2.3 11.3 %copy-start.6 = (f32[2,256,256]{2,1,0:T(8,128)S(1)}, f32[2,256,256]{2,1,0:T(8,128)}, u32[]{:S(2)}) copy-start(f32[2,256,256]{2,1,0:T(8,128)} %param.37) | copy-start | bytes 1572868
  11.4 3.8 collective-permute-start.1
  13.5 243.4 %copy-start.9 = (bf16[1,256,2,256]{1,3,0,2:T(8,128)(2,1)}, bf16[1,256,2,256]{1,3,0,2:T(8,128)(2,1)S(1)}, u32[]{:S(2)}) copy-start(bf16[1,256,2,256]{1,3,0,2:T(8,128)(2,1)S(1)} %get-tuple-element.484) | copy-start | bytes 786436
  13.5 37.0 %copy-start.7 = (bf16[2,256,2,256,1]{1,3,2,0,4:T(8,128)(2,1)}, bf16[2,256,2,256,1]{1,3,2,0,4:T(8,128)(2,1)S(1)}, u32[]{:S(2)}) copy-start(bf16[2,256,2,256,1]{1,3,2,0,4:T(8,128)(2,1)S(1)} %maximum_bitcast_fusion.3) | copy-start | bytes 1572868
  13.6 43.5 %copy-start = (f32[256,256]{1,0:T(8,128)}, f32[256,256]{1,0:T(8,128)S(1)}, u32[]{:S(2)}) copy-start(f32[256,256]{1,0:T(8,128)S(1)} %get-tuple-element.483) | copy-start | bytes 786436
  62.4 0.7 copy-start.8
  177.9 27.4 %collective-permute-start.2 = (f32[2,512,256]{2,1,0:T(8,128)S(1)}, f32[2,512,256]{2,1,0:T(8,128)S(1)}, u32[]{:S(2)}, u32[]{:S(2)}) collective-permute-start(f32[2,512,256]{2,1,0:T(8,128)S(1)} %slice.271), channel_id=1, source_target_pairs={{0,1},{1,2},{2,3},{3,4},{4,5},{5,6},{6,7},{8,9},{9,10},{10,11},{11... | collective-permute-start | bytes 3145736 | tf_op jit(solution)/shard_map/ppermute | solution.py:10
  205.5 5.7 collective-permute-start.3
  211.3 8.4 %collective-permute-start.4 = (bf16[2,256,256]{2,1,0:T(8,128)(2,1)S(1)}, bf16[2,256,256]{2,1,0:T(8,128)(2,1)S(1)}, u32[]{:S(2)}, u32[]{:S(2)}) collective-permute-start(bf16[2,256,256]{2,1,0:T(8,128)(2,1)S(1)} %get-tuple-element.456), channel_id=1, source_target_pairs={{1,0},{2,1},{3,2},{4,3},{5,4},{6,5},{7,6},{9,8},{10,9},{11,10},{12... | collective-permute-start | bytes 786440 | tf_op jit(solution)/shard_map/ppermute | solution.py:10
  219.8 9.5 %collective-permute-start.5 = (bf16[2,256,512]{2,1,0:T(8,128)(2,1)S(1)}, bf16[2,256,512]{2,1,0:T(8,128)(2,1)S(1)}, u32[]{:S(2)}, u32[]{:S(2)}) collective-permute-start(bf16[2,256,512]{2,1,0:T(8,128)(2,1)S(1)} %pad_maximum_fusion.4), channel_id=1, source_target_pairs={{8,0},{16,8},{24,16},{9,1},{17,9},{25,17},{10,2},{18,10},{26,18},{... | collective-permute-start | bytes 1572872 | tf_op jit(solution)/shard_map/ppermute | solution.py:10
  255.3 1.0 copy-start.1
  393.7 24.9 %collective-permute-start.6 = (f32[2,512,256]{2,1,0:T(8,128)S(1)}, f32[2,512,256]{2,1,0:T(8,128)S(1)}, u32[]{:S(2)}, u32[]{:S(2)}) collective-permute-start(f32[2,512,256]{2,1,0:T(8,128)S(1)} %slice.281), channel_id=1, source_target_pairs={{0,1},{1,2},{2,3},{3,4},{4,5},{5,6},{6,7},{8,9},{9,10},{10,11},{11... | collective-permute-start | bytes 3145736 | tf_op jit(solution)/shard_map/ppermute | solution.py:10
  418.8 1.0 copy-start.5
  419.8 8.2 %collective-permute-start.7 = (f32[2,256,256]{2,1,0:T(8,128)S(1)}, f32[2,256,256]{2,1,0:T(8,128)S(1)}, u32[]{:S(2)}, u32[]{:S(2)}) collective-permute-start(f32[2,256,256]{2,1,0:T(8,128)S(1)} %slice.354), channel_id=1, source_target_pairs={{0,8},{8,16},{16,24},{1,9},{9,17},{17,25},{2,10},{10,18},{18,26},{... | collective-permute-start | bytes 1572872 | tf_op jit(solution)/shard_map/ppermute | solution.py:10
  429.9 75.5 %copy-start.3 = (f32[2,256,256]{2,1,0:T(8,128)}, f32[2,256,256]{2,1,0:T(8,128)S(1)}, u32[]{:S(2)}) copy-start(f32[2,256,256]{2,1,0:T(8,128)S(1)} %get-tuple-element.455) | copy-start | bytes 1572868
  490.0 10.4 %collective-permute-start.8 = (bf16[2,256,256]{2,1,0:T(8,128)(2,1)S(1)}, bf16[2,256,256]{2,1,0:T(8,128)(2,1)S(1)}, u32[]{:S(2)}, u32[]{:S(2)}) collective-permute-start(bf16[2,256,256]{2,1,0:T(8,128)(2,1)S(1)} %fusion.86), channel_id=1, source_target_pairs={{1,0},{2,1},{3,2},{4,3},{5,4},{6,5},{7,6},{9,8},{10,9},{11,10},{12... | collective-permute-start | bytes 786440 | tf_op jit(solution)/shard_map/ppermute | solution.py:10
  500.5 3.8 collective-permute-start.9
  530.0 1.0 copy-start.2
  530.9 0.9 copy-start.10
  671.8 33.5 %copy-start.4 = (f32[2,256,256]{2,1,0:T(8,128)S(1)}, f32[2,256,256]{2,1,0:T(8,128)}, u32[]{:S(2)}) copy-start(f32[2,256,256]{2,1,0:T(8,128)} %copy-done.3) | copy-start | bytes 1572868
  671.8 28.4 %collective-permute-start.10 = (f32[2,512,256]{2,1,0:T(8,128)S(1)}, f32[2,512,256]{2,1,0:T(8,128)S(1)}, u32[]{:S(2)}, u32[]{:S(2)}) collective-permute-start(f32[2,512,256]{2,1,0:T(8,128)S(1)} %slice.291), channel_id=1, source_target_pairs={{0,1},{1,2},{2,3},{3,4},{4,5},{5,6},{6,7},{8,9},{9,10},{10,11},{11... | collective-permute-start | bytes 3145736 | tf_op jit(solution)/shard_map/ppermute | solution.py:10
  700.5 4.8 collective-permute-start.11
where the time goes:
time: 758 us; the launch traced here: 757 us
  local copies, waits for them, and re-layouts  306 us (40%)
  blocking collectives  105 us (14%)
  waiting for transfers between devices  98.8 us (13%)
  loops' own time  90.8 us (12%)
  other arithmetic  72.7 us (10%)
  starting transfers between devices  40.7 us (5%)
  matrix products  36.6 us (5%)
    dynamic_update_slice x24, local copies, waits for them, and re-layouts, add_patch(): lax.dynamic_update_slice(running, previous + contribs[k], (anchor, places...  211 us
    ppermute x12, waiting for transfers between devices, from_behind(): return lax.ppermute(block, axis, route)  98.8 us
    another operation x3, loops' own time, accumulate(): return lax.fori_loop(0, contribs.shape[0], add_patch, extended)  90.2 us
    gather x72, local copies, waits for them, and re-layouts  73.4 us
    psum x1, blocking collectives, per_device(): norm_now = lax.psum(jnp.sum(residual * residual), ('ty', 'tx'))  56.1 us
    psum x1, blocking collectives, per_device(): lax.psum(jnp.sum(direction * image_field), ('ty', 'tx'))  48.9 us
    ppermute x12, starting transfers between devices, from_behind(): return lax.ppermute(block, axis, route)  40.7 us
    dot_general x6, matrix products, transform(): jnp.einsum('btrc,trsk->bskc', halfway, tables, preferred_element_type=jnp...  36.6 us
  transfers between devices with their start and end apart: 12, of which 12 were waited for; matrix products, arithmetic and copies ran while one was open for 1% of the time, Pallas kernels for 0%

commit v1 on v0

v1 whole, which is shorter than its diff:
```python
import functools

import jax
import jax.numpy as jnp
import numpy as np
from jax import lax
from jax.experimental import pallas as pl
from jax.experimental.pallas import tpu as pltpu
from jax.sharding import PartitionSpec as P

MESH = pl.DeviceIdType.MESH
LANES = 128
SCALE = 2.0**-24
F32 = jnp.float32
BF16 = jnp.bfloat16
VMEM_SPEC = pl.BlockSpec(memory_space=pltpu.VMEM)
SMEM_SPEC = pl.BlockSpec(memory_space=pltpu.SMEM)


def make_table(extent, direction_sign):
    indices = np.arange(extent)
    angles = (indices[:, None] * indices[None, :] % extent) * (2.0 * np.pi / extent)
    cosine = np.cos(angles) / extent**0.5
    sines = direction_sign * np.sin(angles) / extent**0.5
    table = np.block([[cosine, sines], [-sines, cosine]])
    return jnp.asarray(table.astype(np.float32)).astype(BF16)


def place():
    ty, tx = lax.axis_index("ty"), lax.axis_index("tx")
    return ty, tx, ty > 0, ty < lax.axis_size("ty") - 1, tx > 0, tx < lax.axis_size("tx") - 1


def greet_neighbours():
    ty, tx, has_up, has_down, has_left, has_right = place()
    barrier = pltpu.get_barrier_semaphore()
    sides = (
        (has_up, {"ty": ty - 1}),
        (has_down, {"ty": ty + 1}),
        (has_left, {"tx": tx - 1}),
        (has_right, {"tx": tx + 1}),
    )
    for present, peer in sides:
        @pl.when(present)
        def _():
            pl.semaphore_signal(barrier, inc=1, device_id=peer, device_id_type=MESH)
    pl.semaphore_wait(barrier, sum(present.astype(jnp.int32) for present, _ in sides))


def remote(src, dst, send_sem, recv_sem, index, peer):
    return pltpu.make_async_remote_copy(
        src_ref=src,
        dst_ref=dst,
        send_sem=send_sem.at[index],
        recv_sem=recv_sem.at[index],
        device_id=peer,
        device_id_type=MESH,
    )


def gather_margins(own, right, below, corner, send_sem, recv_sem, base):
    ty, tx, has_up, has_down, has_left, has_right = place()
    to_left = remote(own, right, send_sem, recv_sem, base, {"tx": tx - 1})
    to_up = remote(own, below, send_sem, recv_sem, base + 1, {"ty": ty - 1})
    on_up = remote(right, corner, send_sem, recv_sem, base + 2, {"ty": ty - 1})

    @pl.when(has_left)
    def _():
        to_left.start()

    @pl.when(has_up)
    def _():
        to_up.start()

    @pl.when(has_right)
    def _():
        to_left.wait_recv()

        @pl.when(has_up)
        def _():
            on_up.start()

    @pl.when(has_down)
    def _():
        to_up.wait_recv()

        @pl.when(has_right)
        def _():
            on_up.wait_recv()

    @pl.when(has_left)
    def _():
        to_left.wait_send()

    @pl.when(has_up)
    def _():
        to_up.wait_send()

        @pl.when(has_right)
        def _():
            on_up.wait_send()


def fold_margins(top, bottom, inbox_far, inbox_near, outbox, inbox_side, total, send_sem, recv_sem):
    ty, tx, has_up, has_down, has_left, has_right = place()
    far = remote(bottom.at[pl.ds(2, 2)], inbox_far, send_sem, recv_sem, 0, {"ty": ty + 1})
    near = remote(bottom.at[pl.ds(0, 2)], inbox_near, send_sem, recv_sem, 1, {"ty": ty + 1})
    side = remote(outbox, inbox_side, send_sem, recv_sem, 2, {"tx": tx + 1})

    @pl.when(has_down)
    def _():
        far.start()
        near.start()

    @pl.when(has_up)
    def _():
        far.wait_recv()

        @pl.when(has_right)
        def _():
            outbox[...] = (top[2:4] + inbox_far[...].astype(F32)).astype(BF16)

    @pl.when(jnp.logical_and(ty == 0, has_right))
    def _():
        outbox[...] = top[2:4].astype(BF16)

    @pl.when(has_right)
    def _():
        side.start()

    @pl.when(has_up)
    def _():
        near.wait_recv()
        total[...] = top[0:2] + inbox_near[...].astype(F32)

    @pl.when(ty == 0)
    def _():
        total[...] = top[0:2]

    @pl.when(has_left)
    def _():
        side.wait_recv()
        total[...] += inbox_side[...].astype(F32)

    @pl.when(has_down)
    def _():
        far.wait_send()
        near.wait_send()

    @pl.when(has_right)
    def _():
        side.wait_send()


def spread_kernel(object_ref, own, right, below, corner, send_sem, recv_sem):
    greet_neighbours()
    for h in range(2):
        for t in range(2):
            own[h, t] = object_ref[t, :, h * LANES:(h + 1) * LANES]
    gather_margins(own, right, below, corner, send_sem, recv_sem, 0)


def exchange_first_kernel(top, bottom, q_ref, own, right, below, corner,
                          inbox_far, inbox_near, outbox, inbox_side, total, send_sem, recv_sem):
    greet_neighbours()
    fold_margins(top, bottom, inbox_far, inbox_near, outbox, inbox_side, total, send_sem, recv_sem)
    q = -2.0 * total[...]
    q_ref[...] = q
    own[...] = q.astype(BF16)
    gather_margins(own, right, below, corner, send_sem, recv_sem, 3)


def exchange_kernel(damping, top, bottom, before, q_ref, own, right, below, corner,
                    inbox_far, inbox_near, outbox, inbox_side, total, send_sem, recv_sem):
    greet_neighbours()
    fold_margins(top, bottom, inbox_far, inbox_near, outbox, inbox_side, total, send_sem, recv_sem)
    q = (4.0 * SCALE) * total[...] + (damping[0] * SCALE) * before[...]
    q_ref[...] = q
    own[...] = q.astype(BF16)
    gather_margins(own, right, below, corner, send_sem, recv_sem, 3)


def lane_sums(values):
    return jnp.sum(values.reshape(-1, LANES), 0, keepdims=True)


def finish_kernel(damping, top, bottom, q0_ref, q1_ref, out_ref,
                  inbox_far, inbox_near, outbox, inbox_side, total, sums_y, sums_x,
                  send_sem, recv_sem, send_y, recv_y, send_x, recv_x):
    ty, tx, has_up, has_down, has_left, has_right = place()
    n_y, n_x = lax.axis_size("ty"), lax.axis_size("tx")
    barrier = pltpu.get_barrier_semaphore()
    for axis, me, n in (("ty", ty, n_y), ("tx", tx, n_x)):
        for step in range(1, n):
            pl.semaphore_signal(
                barrier, inc=1, device_id={axis: lax.rem(me + step, n)}, device_id_type=MESH
            )
    pl.semaphore_wait(barrier, n_y + n_x - 2)
    fold_margins(top, bottom, inbox_far, inbox_near, outbox, inbox_side, total, send_sem, recv_sem)
    q0, q1 = q0_ref[...], q1_ref[...]
    q2 = (4.0 * SCALE) * total[...] + (damping[0] * SCALE) * q1
    rows = [lane_sums(q0 * q0), lane_sums(q0 * q1), lane_sums(q1 * q1), lane_sums(q0 * q2), lane_sums(q1 * q2)]
    partial = jnp.concatenate(rows + [jnp.zeros((3, LANES), F32)], 0)

    def reduce_over(partial, sums, send, recv, axis, me, n):
        sums[me] = partial
        copies = []
        for step in range(1, n):
            copies.append(pltpu.make_async_remote_copy(
                src_ref=sums.at[me], dst_ref=sums.at[me],
                send_sem=send.at[step], recv_sem=recv.at[step],
                device_id={axis: lax.rem(me + step, n)}, device_id_type=MESH,
            ))
        for copy in copies:
            copy.start()
        for copy in copies:
            copy.wait()
        return jnp.sum(sums[...], 0)

    partial = reduce_over(partial, sums_y, send_y, recv_y, "ty", ty, n_y)
    partial = reduce_over(partial, sums_x, send_x, recv_x, "tx", tx, n_x)
    dots = jnp.sum(partial, 1, keepdims=True)
    rr, c01, s11, s02, s12 = (dots[k:k + 1] for k in range(5))
    alpha = rr / c01
    rr_next = rr - 2.0 * alpha * c01 + alpha * alpha * s11
    gain = 1.0 + rr_next / rr
    curvature = gain * gain * c01 - gain * alpha * (s02 + s11) + alpha * alpha * s12
    step_len = rr_next / curvature
    first = (alpha + step_len * gain) * SCALE
    second = step_len * alpha * SCALE
    for h in range(2):
        for t in range(2):
            out_ref[t, :, h * LANES:(h + 1) * LANES] = first * q0_ref[h, t] - second * q1_ref[h, t]


def sweep_kernel(first, group, corners, count, own, right, below, corner, probe, table_f, table_g, extra,
                 top, bottom, *rest):
    if first:
        psi_ref, field, total = rest
    else:
        field, total = rest
        psi_ref = extra
    extent = probe.shape[-1]
    tile = own.shape[2]
    slots = psi_ref.shape[0]
    field[0:2, :, 0:tile] = own[...].astype(F32)
    field[2:4, :, 0:tile] = right[...].astype(F32)
    field[0:2, :, tile:] = below[...].astype(F32)
    field[2:4, :, tile:] = corner[...].astype(F32)
    total[...] = jnp.zeros_like(total)
    lane = lax.broadcasted_iota(jnp.int32, (extent, LANES), 1)
    live = count[0]

    def cut(s):
        row, col = corners[s, 0], corners[s, 1]
        block, shift = col // LANES, lax.rem(col, LANES)
        keep = lane < LANES - shift
        halves = []
        for t in range(2):
            turned = [
                pltpu.roll(field[block + k, t, pl.ds(row, extent), :], lax.rem(LANES - shift, LANES), 1)
                for k in range(3)
            ]
            halves.append([jnp.where(keep, turned[k], turned[k + 1]) for k in range(2)])
        waves = [[], []]
        for k in range(2):
            probe_re = probe[0, :, k * LANES:(k + 1) * LANES]
            probe_im = probe[1, :, k * LANES:(k + 1) * LANES]
            waves[0].append((probe_re * halves[0][k] - probe_im * halves[1][k]).astype(BF16))
            waves[1].append((probe_re * halves[1][k] + probe_im * halves[0][k]).astype(BF16))
        return jnp.concatenate(waves[0] + waves[1], 1)

    def add(s, back):
        row, col = corners[s, 0], corners[s, 1]
        block, shift = col // LANES, lax.rem(col, LANES)
        keep = lane >= shift
        back = back.astype(BF16).astype(F32)
        for t in range(2):
            turned = []
            for k in range(2):
                lanes = slice(k * LANES, (k + 1) * LANES)
                probe_re, probe_im = probe[0, :, lanes], probe[1, :, lanes]
                re, im = back[:extent, lanes], back[extent:, lanes]
                if t == 0:
                    term = probe_re * re + probe_im * im
                else:
                    term = probe_re * im - probe_im * re
                turned.append(pltpu.roll(term, shift, 1))
            zero = jnp.zeros_like(turned[0])
            pieces = [
                jnp.where(keep, turned[0], zero),
                jnp.where(keep, turned[1], turned[0]),
                jnp.where(keep, zero, turned[1]),
            ]
            for k in range(3):
                total[block + k, t, pl.ds(row, extent), :] += pieces[k]

    def transform(waves, rhs, lhs):
        half = jnp.dot(waves, rhs[...], preferred_element_type=F32).astype(BF16)
        columns = []
        for g in range(group):
            part = half[g * extent:(g + 1) * extent]
            columns.append(jnp.concatenate([part[:, :extent], part[:, extent:]], 0))
        return jnp.dot(lhs[...], jnp.concatenate(columns, 1), preferred_element_type=F32)

    def step(index, carry):
        base = index * group
        waves = jnp.concatenate([cut(base + g) for g in range(group)], 0)
        image = transform(waves, table_f, table_g)
        mixed = []
        for g in range(group):
            re = image[:extent, g * extent:(g + 1) * extent]
            im = image[extent:, g * extent:(g + 1) * extent]
            if first:
                psi_ref[base + g, 0] = re
                psi_ref[base + g, 1] = im
                weight = re * re + im * im - extra[base + g].astype(F32)
                psi_re, psi_im = re, im
            else:
                psi_re, psi_im = psi_ref[base + g, 0], psi_ref[base + g, 1]
                weight = psi_re * re + psi_im * im
            mixed.append(jnp.concatenate([(psi_re * weight).astype(BF16), (psi_im * weight).astype(BF16)], 1))
        back = transform(jnp.concatenate(mixed, 0), table_g, table_f)
        for g in range(group):
            @pl.when(base + g < live)
            def _():
                add(base + g, back[:, g * extent:(g + 1) * extent])
        return carry

    lax.fori_loop(0, (live + group - 1) // group, step, 0)
    top[...] = total[:, :, 0:tile]
    bottom[...] = total[:, :, tile:].astype(BF16)


def per_device(object_field, probe_field, corners, counts, intensity, damping):
    extent = probe_field.shape[-1]
    tile = object_field.shape[1]
    slots = corners.shape[2]
    group = 2
    n_y, n_x = lax.axis_size("ty"), lax.axis_size("tx")
    places = corners.reshape(slots, 2)
    count = counts.reshape(1)
    measured = intensity.reshape(slots, extent, extent)
    damping = damping.reshape(1)
    table_f, table_g = make_table(extent, -1.0), make_table(extent, 1.0)

    def shaped(shape, dtype):
        return jax.ShapeDtypeStruct(shape, dtype)

    quarter = (2, 2, tile, LANES)
    quarters = [shaped(quarter, BF16)] * 4
    boxes = [pltpu.VMEM(quarter, BF16)] * 4 + [pltpu.VMEM(quarter, F32)]

    def sems(n):
        return [pltpu.SemaphoreType.DMA((n,)), pltpu.SemaphoreType.DMA((n,))]

    def params(collective_id):
        return pltpu.CompilerParams(
            collective_id=collective_id, has_side_effects=True, vmem_limit_bytes=16 << 20
        )

    margins = pl.pallas_call(
        spread_kernel,
        out_shape=quarters,
        in_specs=[VMEM_SPEC],
        out_specs=[VMEM_SPEC] * 4,
        scratch_shapes=sems(3),
        compiler_params=params(0),
        name="spread",
    )(object_field)

    def sweep(margins, extra, first):
        outs = [shaped((4, 2, tile, LANES), F32), shaped((4, 2, tile, LANES), BF16)]
        if first:
            outs.append(shaped((slots, 2, extent, extent), F32))
        return pl.pallas_call(
            functools.partial(sweep_kernel, first, group),
            out_shape=outs,
            in_specs=[SMEM_SPEC] * 2 + [VMEM_SPEC] * 8,
            out_specs=[VMEM_SPEC] * len(outs),
            scratch_shapes=[pltpu.VMEM((4, 2, 2 * tile, LANES), F32)] * 2,
            compiler_params=pltpu.CompilerParams(vmem_limit_bytes=36 << 20),
            name="sweep_first" if first else "sweep",
        )(places, count, *margins, probe_field, table_f, table_g, extra)

    top, bottom, psi = sweep(margins, measured, True)
    q0, *margins = pl.pallas_call(
        exchange_first_kernel,
        out_shape=[shaped(quarter, F32)] + quarters,
        in_specs=[VMEM_SPEC] * 2,
        out_specs=[VMEM_SPEC] * 5,
        scratch_shapes=boxes + sems(6),
        compiler_params=params(1),
        name="exchange_first",
    )(top, bottom)
    top, bottom = sweep(margins, psi, False)
    q1, *margins = pl.pallas_call(
        exchange_kernel,
        out_shape=[shaped(quarter, F32)] + quarters,
        in_specs=[SMEM_SPEC] + [VMEM_SPEC] * 3,
        out_specs=[VMEM_SPEC] * 5,
        scratch_shapes=boxes + sems(6),
        compiler_params=params(2),
        name="exchange",
    )(damping, top, bottom, q0)
    top, bottom = sweep(margins, psi, False)
    return pl.pallas_call(
        finish_kernel,
        out_shape=shaped((2, tile, tile), F32),
        in_specs=[SMEM_SPEC] + [VMEM_SPEC] * 4,
        out_specs=VMEM_SPEC,
        scratch_shapes=boxes
        + [pltpu.VMEM((n_y, 8, LANES), F32), pltpu.VMEM((n_x, 8, LANES), F32)]
        + sems(3) + sems(n_y) + sems(n_x),
        compiler_params=params(3),
        name="finish",
    )(damping, top, bottom, q0, q1)


def solution(mesh):
    in_specs = (
        P(None, "ty", "tx"),
        P(),
        P("ty", "tx", None, None),
        P("ty", "tx"),
        P("ty", "tx", None, None, None),
        P(),
    )
    out_specs = P(None, "ty", "tx")
    return jax.shard_map(
        per_device, mesh=mesh, in_specs=in_specs, out_specs=out_specs, check_vma=False
    )
```

time: 758 us -> 125 us (0.16)
  local copies, waits for them, and re-layouts: 306 us -> 6.85 us
  Pallas kernels: 0 us -> 115 us
  blocking collectives: 105 us -> 0 us
  waiting for transfers between devices: 98.8 us -> 0 us
  loops' own time: 90.8 us -> 0 us
  other arithmetic: 72.7 us -> 0 us
  starting transfers between devices: 40.7 us -> 0 us
  matrix products: 36.6 us -> 0 us
    dynamic_update_slice x24 -> x0, local copies, waits for them, and re-layouts: 211 us -> none  [add_patch(): lax.dynamic_update_slice(running, previous + contribs[k], (anchor, places...]
    pallas_call x0 -> x7, Pallas kernels: none -> 115 us  [the longest x3 30 us: sweep(): pl.pallas_call(functools.partial(sweep_kernel, first, group), out_shape=o...]
    psum x2 -> x0, blocking collectives: 105 us -> none  [the longest x1 56.1 us: per_device(): norm_now = lax.psum(jnp.sum(residual * residual), ('ty', 'tx'))]
    ppermute x12 -> x0, waiting for transfers between devices: 98.8 us -> none  [from_behind(): return lax.ppermute(block, axis, route)]
    another operation x6 -> x0, loops' own time: 90.8 us -> none  [the longest x3 90.2 us: accumulate(): return lax.fori_loop(0, contribs.shape[0], add_patch, extended)]
    gather x72 -> x0, local copies, waits for them, and re-layouts: 73.4 us -> none
    ppermute x12 -> x0, starting transfers between devices: 40.7 us -> none  [from_behind(): return lax.ppermute(block, axis, route)]
    add x31 -> x0, other arithmetic: 40.1 us -> none  [the longest x24 30.3 us: add_patch(): previous + contribs[k]]
  transfers between devices with their start and end apart: 12 -> 0, of which waited for: 12 -> 0; matrix products, arithmetic and copies ran while one was open for 1% -> 0% of each run, Pallas kernels for 0% -> 0%
where the time goes in v1:
time: 125 us; the launch traced here: 123 us
  Pallas kernels  115 us (92%)
  local copies, waits for them, and re-layouts  6.85 us (5%)
  between operations  1.37 us (1%)
    pallas_call x3, Pallas kernels, sweep(): pl.pallas_call(functools.partial(sweep_kernel, first, group), out_shape=o...  30 us
    pallas_call x1, Pallas kernels, per_device(): pl.pallas_call(finish_kernel, out_shape=shaped((2, tile, tile), F32), in_...  26.8 us
    pallas_call x1, Pallas kernels, per_device(): pl.pallas_call(exchange_kernel, out_shape=[shaped(quarter, F32)] + quarte...  25.9 us
    pallas_call x1, Pallas kernels, per_device(): pl.pallas_call(exchange_first_kernel, out_shape=[shaped(quarter, F32)] +...  20.1 us
    pallas_call x1, Pallas kernels, per_device(): pl.pallas_call(spread_kernel, out_shape=quarters, in_specs=[VMEM_SPEC], o...  11.7 us
    unnamed x13, local copies, waits for them, and re-layouts  6.09 us

profile of v1, /device:TPU:0, one launch (start us, length us, event | category | flops | bytes accessed | tf_op | source)
XLA Modules:
  0.0 122.8 jit_solution(17068290582591078531)
XLA Ops:
  1.3 0.8 copy.11.corners
  2.1 0.0 copy-start.5
  2.1 0.9 copy-done.5
  3.0 11.7 %spread.1 = (bf16[2,2,256,128]{3,2,1,0:T(8,128)(2,1)S(1)}, bf16[2,2,256,128]{3,2,1,0:T(8,128)(2,1)S(1)}, bf16[2,2,256,128]{3,2,1,0:T(8,128)(2,1)S(1)}, bf16[2,2,256,128]{3,2,1,0:T(8,128)(2,1)S(1)}) custom-call(bf16[2,256,256]{2,1,0:T(8,128)(2,1)S(1)} %copy-done.5), custom_call_target="tpu_custom_call" | custom-call | tf_op jit(solution)/shard_map/spread/pallas_call | solution.py:362
  14.7 0.0 copy-start
  14.8 1.0 copy-done
  15.8 0.0 copy-start.2
  15.8 1.0 copy-done.2
  16.8 0.0 copy-start.3
  16.8 1.0 copy-done.3
  17.9 0.0 copy-start.4
  17.9 1.2 copy-done.4
  19.1 0.0 copy-start.1
  19.1 10.0 %sweep_first.1 = (f32[4,2,256,128]{3,2,1,0:T(8,128)S(1)}, bf16[4,2,256,128]{3,2,1,0:T(8,128)(2,1)S(1)}, f32[8,2,256,256]{3,2,1,0:T(8,128)S(1)}) custom-call(s32[8,2]{1,0:T(8,128)S(1)} %copy.11.corners, s32[1]{0:T(128)} %bitcast.4.count, bf16[2,2,256,128]{3,2,1,0:T(8,128)(2,1)S(1)} %get-tuple-element.26.own, ...), custom_call_target="tpu_custom_call" | custom-call | tf_op jit(solution)/shard_map/sweep_first/pallas_call | solution.py:376
  29.1 20.1 %exchange_first.1 = (f32[2,2,256,128]{3,2,1,0:T(8,128)S(1)}, bf16[2,2,256,128]{3,2,1,0:T(8,128)(2,1)S(1)}, bf16[2,2,256,128]{3,2,1,0:T(8,128)(2,1)S(1)}, bf16[2,...) custom-call(f32[4,2,256,128]{3,2,1,0:T(8,128)S(1)} %get-tuple-element.30.top, ...), custom_call_target="tpu_custom_call" | custom-call | tf_op jit(solution)/shard_map/exchange_first/pallas_call | solution.py:387
  49.2 0.0 copy-done.1
  49.3 10.0 %sweep.2 = (f32[4,2,256,128]{3,2,1,0:T(8,128)S(1)}, bf16[4,2,256,128]{3,2,1,0:T(8,128)(2,1)S(1)}) custom-call(s32[8,2]{1,0:T(8,128)S(1)} %copy.11.corners, s32[1]{0:T(128)} %bitcast.5.count, bf16[2,2,256,128]{3,2,1,0:T(8,128)(2,1)S(1)} %get-tuple-element.32.own, bf16[2,2,256,128]{3,2,1,0:T(8,128)(2,1)S(1)} %get-tuple-element.33.right, ...), custom_call_target="tpu_custom_call" | custom-call | tf_op jit(solution)/shard_map/sweep/pallas_call | solution.py:376
  59.3 25.9 %exchange.1 = (f32[2,2,256,128]{3,2,1,0:T(8,128)S(1)}, bf16[2,2,256,128]{3,2,1,0:T(8,128)(2,1)S(1)}, bf16[2,2,256,128]{3,2,1,0:T(8,128)(2,1)S(1)}, bf16[2,2,256,...) custom-call(f32[1]{0:T(128)} %bitcast.7.damping, f32[4,2,256,128]{3,2,1,0:T(8,128)S(1)} %get-tuple-element.37.top, ...), custom_call_target="tpu_custom_call" | custom-call | tf_op jit(solution)/shard_map/exchange/pallas_call | solution.py:397
  85.2 10.0 %sweep.3 = (f32[4,2,256,128]{3,2,1,0:T(8,128)S(1)}, bf16[4,2,256,128]{3,2,1,0:T(8,128)(2,1)S(1)}) custom-call(s32[8,2]{1,0:T(8,128)S(1)} %copy.11.corners, s32[1]{0:T(128)} %bitcast.6.count, bf16[2,2,256,128]{3,2,1,0:T(8,128)(2,1)S(1)} %get-tuple-element.40.own, bf16[2,2,256,128]{3,2,1,0:T(8,128)(2,1)S(1)} %get-tuple-element.41.right, ...), custom_call_target="tpu_custom_call" | custom-call | tf_op jit(solution)/shard_map/sweep/pallas_call | solution.py:376
  95.2 26.8 %finish.1 = f32[2,256,256]{2,1,0:T(8,128)S(1)} custom-call(f32[1]{0:T(128)} %bitcast.8.damping, f32[4,2,256,128]{3,2,1,0:T(8,128)S(1)} %get-tuple-element.44.top, bf16[4,2,256,128]{3,2,1,0:T(8,128)(2,1)S(1)} %get-tuple-element.45.bottom, f32[2,2,256,128]{3,2,1,0:T(8,128)S(1)} %get-tuple-element.39.before.q0_ref, f32[2,2,256,128]{3,2,1,0:T(8,128)S(1)} %get-tuple-element.46.q1_ref), custom_call_target="tpu_custom_call" | custom-call | tf_op jit(solution)/shard_map/finish/pallas_call | solution.py:407
  122.0 0.8 copy.15
Async XLA Ops:
  2.1 0.9 copy-start.5
  14.7 1.0 copy-start
  15.8 1.0 copy-start.2
  16.8 1.0 copy-start.3
  17.9 1.2 copy-start.4
  19.1 30.2 %copy-start.1 = (f32[2,256,256]{2,1,0:T(8,128)S(1)}, f32[2,256,256]{2,1,0:T(8,128)}, u32[]{:S(2)}) copy-start(f32[2,256,256]{2,1,0:T(8,128)} %probe.5) | copy-start | bytes 1572868

commit v2 on v1

--- a/solution.py
+++ b/solution.py
@@ -11,6 +11,7 @@
 MESH = pl.DeviceIdType.MESH
 LANES = 128
 SCALE = 2.0**-24
+CHUNKS = 4
 F32 = jnp.float32
 BF16 = jnp.bfloat16
 VMEM_SPEC = pl.BlockSpec(memory_space=pltpu.VMEM)
@@ -58,126 +59,193 @@
     )
 
 
-def gather_margins(own, right, below, corner, send_sem, recv_sem, base):
+def rows_of(chunk, extent):
+    size = extent // CHUNKS
+    return pl.ds(chunk * size, size)
+
+
+def margin_copies(own, right, below, corner, send_sem, recv_sem, base):
+    ty, tx = place()[:2]
+    to_left, to_up, on_up = [], [], []
+    for c in range(CHUNKS):
+        rows = rows_of(c, own.shape[2])
+        part = [ref.at[:, :, rows] for ref in (own, right, below, corner)]
+        to_left.append(remote(part[0], part[1], send_sem, recv_sem, base + 3 * c, {"tx": tx - 1}))
+        to_up.append(remote(part[0], part[2], send_sem, recv_sem, base + 3 * c + 1, {"ty": ty - 1}))
+        on_up.append(remote(part[1], part[3], send_sem, recv_sem, base + 3 * c + 2, {"ty": ty - 1}))
+    return to_left, to_up, on_up
+
+
+def send_margins(copies, c):
     ty, tx, has_up, has_down, has_left, has_right = place()
-    to_left = remote(own, right, send_sem, recv_sem, base, {"tx": tx - 1})
-    to_up = remote(own, below, send_sem, recv_sem, base + 1, {"ty": ty - 1})
-    on_up = remote(right, corner, send_sem, recv_sem, base + 2, {"ty": ty - 1})
+    to_left, to_up, on_up = copies
 
     @pl.when(has_left)
     def _():
-        to_left.start()
+        to_left[c].start()
 
     @pl.when(has_up)
     def _():
-        to_up.start()
+        to_up[c].start()
+
+
+def settle_margins(copies):
+    ty, tx, has_up, has_down, has_left, has_right = place()
+    to_left, to_up, on_up = copies
 
     @pl.when(has_right)
     def _():
-        to_left.wait_recv()
-
+        for c in range(CHUNKS):
+            to_left[c].wait_recv()
+
+            @pl.when(has_up)
+            def _():
+                on_up[c].start()
+
+    @pl.when(has_down)
+    def _():
+        for copy in to_up:
+            copy.wait_recv()
+
+        @pl.when(has_right)
+        def _():
+            for copy in on_up:
+                copy.wait_recv()
+
+    @pl.when(has_left)
+    def _():
+        for copy in to_left:
+            copy.wait_send()
+
+    @pl.when(has_up)
+    def _():
+        for copy in to_up:
+            copy.wait_send()
+
+        @pl.when(has_right)
+        def _():
+            for copy in on_up:
+                copy.wait_send()
+
+
+def fold_margins(top, bottom, inbox_far, inbox_near, outbox, inbox_side, total, send_sem, recv_sem, use):
+    ty, tx, has_up, has_down, has_left, has_right = place()
+    far, near, side, spans = [], [], [], []
+    for c in range(CHUNKS):
+        rows = rows_of(c, total.shape[2])
+        spans.append(rows)
+        far.append(remote(
+            bottom.at[pl.ds(2, 2), :, rows], inbox_far.at[:, :, rows], send_sem, recv_sem, 3 * c, {"ty": ty + 1}
+        ))
+        near.append(remote(
+            bottom.at[pl.ds(0, 2), :, rows], inbox_near.at[:, :, rows], send_sem, recv_sem, 3 * c + 1, {"ty": ty + 1}
+        ))
+        side.append(remote(
+            outbox.at[:, :, rows], inbox_side.at[:, :, rows], send_sem, recv_sem, 3 * c + 2, {"tx": tx + 1}
+        ))
+
+    @pl.when(has_down)
+    def _():
+        for copy in far + near:
+            copy.start()
+
+    for c in range(CHUNKS):
         @pl.when(has_up)
         def _():
-            on_up.start()
+            far[c].wait_recv()
+
+            @pl.when(has_right)
+            def _():
+                outbox[:, :, spans[c]] = (
+                    top[2:4, :, spans[c]] + inbox_far[:, :, spans[c]].astype(F32)
+                ).astype(BF16)
+
+        @pl.when(jnp.logical_and(ty == 0, has_right))
+        def _():
+            outbox[:, :, spans[c]] = top[2:4, :, spans[c]].astype(BF16)
+
+        @pl.when(has_right)
+        def _():
+            side[c].start()
+
+    for c in range(CHUNKS):
+        @pl.when(has_up)
+        def _():
+            near[c].wait_recv()
+            total[:, :, spans[c]] = top[0:2, :, spans[c]] + inbox_near[:, :, spans[c]].astype(F32)
+
+        @pl.when(ty == 0)
+        def _():
+            total[:, :, spans[c]] = top[0:2, :, spans[c]]
+
+        @pl.when(has_left)
+        def _():
+            side[c].wait_recv()
+            total[:, :, spans[c]] += inbox_side[:, :, spans[c]].astype(F32)
+
+        use(c, spans[c])
 
     @pl.when(has_down)
     def _():
-        to_up.wait_recv()
-
-        @pl.when(has_right)
-        def _():
-            on_up.wait_recv()
-
-    @pl.when(has_left)
-    def _():
-        to_left.wait_send()
-
-    @pl.when(has_up)
-    def _():
-        to_up.wait_send()
-
-        @pl.when(has_right)
-        def _():
-            on_up.wait_send()
-
-
-def fold_margins(top, bottom, inbox_far, inbox_near, outbox, inbox_side, total, send_sem, recv_sem):
-    ty, tx, has_up, has_down, has_left, has_right = place()
-    far = remote(bottom.at[pl.ds(2, 2)], inbox_far, send_sem, recv_sem, 0, {"ty": ty + 1})
-    near = remote(bottom.at[pl.ds(0, 2)], inbox_near, send_sem, recv_sem, 1, {"ty": ty + 1})
-    side = remote(outbox, inbox_side, send_sem, recv_sem, 2, {"tx": tx + 1})
-
-    @pl.when(has_down)
-    def _():
-        far.start()
-        near.start()
-
-    @pl.when(has_up)
-    def _():
-        far.wait_recv()
-
-        @pl.when(has_right)
-        def _():
-            outbox[...] = (top[2:4] + inbox_far[...].astype(F32)).astype(BF16)
-
-    @pl.when(jnp.logical_and(ty == 0, has_right))
-    def _():
-        outbox[...] = top[2:4].astype(BF16)
+        for copy in far + near:
+            copy.wait_send()
 
     @pl.when(has_right)
     def _():
-        side.start()
-
-    @pl.when(has_up)
-    def _():
-        near.wait_recv()
-        total[...] = top[0:2] + inbox_near[...].astype(F32)
-
-    @pl.when(ty == 0)
-    def _():
-        total[...] = top[0:2]
-
-    @pl.when(has_left)
-    def _():
-        side.wait_recv()
-        total[...] += inbox_side[...].astype(F32)
-
-    @pl.when(has_down)
-    def _():
-        far.wait_send()
-        near.wait_send()
-
-    @pl.when(has_right)
-    def _():
-        side.wait_send()
-
-
-def spread_kernel(object_ref, own, right, below, corner, send_sem, recv_sem):
+        for copy in side:
+            copy.wait_send()
+
+
+def spread_kernel(object_ref, *refs):
+    sources, (own, right, below, corner), targets = refs[:4], refs[4:8], refs[8:12]
+    send_sem, recv_sem, load_sem = refs[12:]
+    loads = [
+        pltpu.make_async_copy(
+            object_ref.at[t, :, pl.ds(h * LANES, LANES)], own.at[h, t], load_sem.at[2 * h + t]
+        )
+        for h in range(2) for t in range(2)
+    ]
+    stages = [
+        pltpu.make_async_copy(source, target, load_sem.at[4 + k])
+        for k, (source, target) in enumerate(zip(sources, targets))
+    ]
+    for copy in loads + stages:
+        copy.start()
     greet_neighbours()
-    for h in range(2):
-        for t in range(2):
-            own[h, t] = object_ref[t, :, h * LANES:(h + 1) * LANES]
-    gather_margins(own, right, below, corner, send_sem, recv_sem, 0)
-
-
-def exchange_first_kernel(top, bottom, q_ref, own, right, below, corner,
-                          inbox_far, inbox_near, outbox, inbox_side, total, send_sem, recv_sem):
+    for copy in loads:
+        copy.wait()
+    copies = margin_copies(own, right, below, corner, send_sem, recv_sem, 0)
+    for c in range(CHUNKS):
+        send_margins(copies, c)
+    settle_margins(copies)
+    for copy in stages:
+        copy.wait()
+
+
+def exchange_kernel(first, *refs):
+    if first:
+        top, bottom = refs[:2]
+        refs = refs[2:]
+    else:
+        damping, top, bottom, before = refs[:4]
+        refs = refs[4:]
+    q_ref, own, right, below, corner = refs[:5]
+    boxes, (send_sem, recv_sem) = refs[5:10], refs[10:]
+    total = boxes[-1]
     greet_neighbours()
-    fold_margins(top, bottom, inbox_far, inbox_near, outbox, inbox_side, total, send_sem, recv_sem)
-    q = -2.0 * total[...]
-    q_ref[...] = q
-    own[...] = q.astype(BF16)
-    gather_margins(own, right, below, corner, send_sem, recv_sem, 3)
-
-
-def exchange_kernel(damping, top, bottom, before, q_ref, own, right, below, corner,
-                    inbox_far, inbox_near, outbox, inbox_side, total, send_sem, recv_sem):
-    greet_neighbours()
-    fold_margins(top, bottom, inbox_far, inbox_near, outbox, inbox_side, total, send_sem, recv_sem)
-    q = (4.0 * SCALE) * total[...] + (damping[0] * SCALE) * before[...]
-    q_ref[...] = q
-    own[...] = q.astype(BF16)
-    gather_margins(own, right, below, corner, send_sem, recv_sem, 3)
+    copies = margin_copies(own, right, below, corner, send_sem, recv_sem, 3 * CHUNKS)
+
+    def use(c, rows):
+        if first:
+            q = -2.0 * total[:, :, rows]
+        else:
+            q = (4.0 * SCALE) * total[:, :, rows] + (damping[0] * SCALE) * before[:, :, rows]
+        q_ref[:, :, rows] = q
+        own[:, :, rows] = q.astype(BF16)
+        send_margins(copies, c)
+
+    fold_margins(top, bottom, *boxes, send_sem, recv_sem, use)
+    settle_margins(copies)
 
 
 def lane_sums(values):
@@ -196,7 +264,8 @@
                 barrier, inc=1, device_id={axis: lax.rem(me + step, n)}, device_id_type=MESH
             )
     pl.semaphore_wait(barrier, n_y + n_x - 2)
-    fold_margins(top, bottom, inbox_far, inbox_near, outbox, inbox_side, total, send_sem, recv_sem)
+    fold_margins(top, bottom, inbox_far, inbox_near, outbox, inbox_side, total, send_sem, recv_sem,
+                 lambda c, rows: None)
     q0, q1 = q0_ref[...], q1_ref[...]
     q2 = (4.0 * SCALE) * total[...] + (damping[0] * SCALE) * q1
     rows = [lane_sums(q0 * q0), lane_sums(q0 * q1), lane_sums(q1 * q1), lane_sums(q0 * q2), lane_sums(q1 * q2)]
@@ -252,7 +321,7 @@
     live = count[0]
 
     def cut(s):
-        row, col = corners[s, 0], corners[s, 1]
+        row, col = corners[0, s], corners[1, s]
         block, shift = col // LANES, lax.rem(col, LANES)
         keep = lane < LANES - shift
         halves = []
@@ -271,7 +340,7 @@
         return jnp.concatenate(waves[0] + waves[1], 1)
 
     def add(s, back):
-        row, col = corners[s, 0], corners[s, 1]
+        row, col = corners[0, s], corners[1, s]
         block, shift = col // LANES, lax.rem(col, LANES)
         keep = lane >= shift
         back = back.astype(BF16).astype(F32)
@@ -338,7 +407,7 @@
     slots = corners.shape[2]
     group = 2
     n_y, n_x = lax.axis_size("ty"), lax.axis_size("tx")
-    places = corners.reshape(slots, 2)
+    places = corners.reshape(slots, 2).T
     count = counts.reshape(1)
     measured = intensity.reshape(slots, extent, extent)
     damping = damping.reshape(1)
@@ -359,15 +428,16 @@
             collective_id=collective_id, has_side_effects=True, vmem_limit_bytes=16 << 20
         )
 
-    margins = pl.pallas_call(
+    staged = (probe_field, table_f, table_g, measured)
+    *margins, probe_field, table_f, table_g, measured = pl.pallas_call(
         spread_kernel,
-        out_shape=quarters,
-        in_specs=[VMEM_SPEC],
-        out_specs=[VMEM_SPEC] * 4,
-        scratch_shapes=sems(3),
+        out_shape=quarters + [shaped(array.shape, array.dtype) for array in staged],
+        in_specs=[pl.BlockSpec(memory_space=pltpu.HBM)] * 5,
+        out_specs=[VMEM_SPEC] * 8,
+        scratch_shapes=sems(3 * CHUNKS) + [pltpu.SemaphoreType.DMA((8,))],
         compiler_params=params(0),
         name="spread",
-    )(object_field)
+    )(object_field, *staged)
 
     def sweep(margins, extra, first):
         outs = [shaped((4, 2, tile, LANES), F32), shaped((4, 2, tile, LANES), BF16)]
@@ -385,21 +455,21 @@
 
     top, bottom, psi = sweep(margins, measured, True)
     q0, *margins = pl.pallas_call(
-        exchange_first_kernel,
+        functools.partial(exchange_kernel, True),
         out_shape=[shaped(quarter, F32)] + quarters,
         in_specs=[VMEM_SPEC] * 2,
         out_specs=[VMEM_SPEC] * 5,
-        scratch_shapes=boxes + sems(6),
+        scratch_shapes=boxes + sems(6 * CHUNKS),
         compiler_params=params(1),
         name="exchange_first",
     )(top, bottom)
     top, bottom = sweep(margins, psi, False)
     q1, *margins = pl.pallas_call(
-        exchange_kernel,
+        functools.partial(exchange_kernel, False),
         out_shape=[shaped(quarter, F32)] + quarters,
         in_specs=[SMEM_SPEC] + [VMEM_SPEC] * 3,
         out_specs=[VMEM_SPEC] * 5,
-        scratch_shapes=boxes + sems(6),
+        scratch_shapes=boxes + sems(6 * CHUNKS),
         compiler_params=params(2),
         name="exchange",
     )(damping, top, bottom, q0)
@@ -411,7 +481,7 @@
         out_specs=VMEM_SPEC,
         scratch_shapes=boxes
         + [pltpu.VMEM((n_y, 8, LANES), F32), pltpu.VMEM((n_x, 8, LANES), F32)]
-        + sems(3) + sems(n_y) + sems(n_x),
+        + sems(3 * CHUNKS) + sems(n_y) + sems(n_x),
         compiler_params=params(3),
         name="finish",
     )(damping, top, bottom, q0, q1)

time: 125 us -> 115 us (0.920); the launches traced: 123 us -> 115 us
  Pallas kernels: 115 us -> 107 us
    pallas_call x3, Pallas kernels: 30 us -> 23.7 us  [sweep(): pl.pallas_call(functools.partial(sweep_kernel, first, group), out_shape=o...]
    pallas_call x1, Pallas kernels: 26.8 us -> 24.6 us  [per_device(): pl.pallas_call(finish_kernel, out_shape=shaped((2, tile, tile), F32), in_...]
where the time goes in v2:
time: 115 us
  Pallas kernels  107 us (93%)
  local copies, waits for them, and re-layouts  6.76 us (6%)
  between operations  1.37 us (1%)
    pallas_call x1, Pallas kernels, per_device(): pl.pallas_call(finish_kernel, out_shape=shaped((2, tile, tile), F32), in_...  24.6 us
    pallas_call x3, Pallas kernels, sweep(): pl.pallas_call(functools.partial(sweep_kernel, first, group), out_shape=o...  23.7 us
    pallas_call x1, Pallas kernels, per_device(): pl.pallas_call(functools.partial(exchange_kernel, False), out_shape=[shap...  23.4 us
    pallas_call x1, Pallas kernels, per_device(): pl.pallas_call(functools.partial(exchange_kernel, True), out_shape=[shape...  23.2 us
    pallas_call x1, Pallas kernels, per_device(): pl.pallas_call(spread_kernel, out_shape=quarters + [shaped(array.shape, a...  11.9 us
    unnamed x13, local copies, waits for them, and re-layouts  6.76 us

profile of v2, /device:TPU:0, one launch (start us, length us, event | category | flops | bytes accessed | tf_op | source)
XLA Modules:
  0.0 114.9 jit_solution(13994817883625735047)
XLA Ops:
  1.3 0.0 copy-start
  1.3 1.2 %copy-done = bf16[1,1,8,256,256]{4,3,2,1,0:T(8,128)(2,1)S(1)} copy-done((bf16[1,1,8,256,256]{4,3,2,1,0:T(8,128)(2,1)S(1)}, bf16[1,1,8,256,256]{4,3,2,1,0:T(8,128)(2,1)}, u32[]{:S(2)}) %copy-start) | copy-done | bytes 1048600
  2.5 0.0 copy-start.1
  2.5 1.0 copy-done.1
  3.6 0.0 copy-start.2
  3.6 1.0 copy-done.2
  4.6 0.0 copy-start.3
  4.6 1.0 copy-done.3
  5.7 0.0 copy-start.4
  5.7 0.9 copy-done.4
  6.6 11.9 %spread.1 = (bf16[2,2,256,128]{3,2,1,0:T(8,128)(2,1)S(1)}, bf16[2,2,256,128]{3,2,1,0:T(8,128)(2,1)S(1)}, bf16[2,2,256,128]{3,2,1,0:T(8,128)(2,1)S(1)}, bf16[2,2,...) custom-call(bf16[2,256,256]{2,1,0:T(8,128)(2,1)S(1)} %copy-done.4, ...), custom_call_target="tpu_custom_call" | custom-call | tf_op jit(solution)/shard_map/spread/pallas_call | solution.py:432
  18.5 0.0 copy-start.5
  18.5 0.7 copy-done.5
  19.2 7.9 %sweep_first.1 = (f32[4,2,256,128]{3,2,1,0:T(8,128)S(1)}, bf16[4,2,256,128]{3,2,1,0:T(8,128)(2,1)S(1)}, f32[8,2,256,256]{3,2,1,0:T(8,128)S(1)}) custom-call(s32[2,8]{1,0:T(2,128)S(1)} %bitcast.12, s32[1]{0:T(128)} %bitcast.6.count, bf16[2,2,256,128]{3,2,1,0:T(8,128)(2,1)S(1)} %get-tuple-element.30.own, bf16[2,2,256,128]{3,2,1,0:T(8,128)(2,1)S(1)} %get-tuple-element.31.right, ...), custom_call_target="tpu_custom_call" | custom-call | tf_op jit(solution)/shard_map/sweep_first/pallas_call | solution.py:446
  27.1 23.2 %exchange_first.1 = (f32[2,2,256,128]{3,2,1,0:T(8,128)S(1)}, bf16[2,2,256,128]{3,2,1,0:T(8,128)(2,1)S(1)}, bf16[2,2,256,128]{3,2,1,0:T(8,128)(2,1)S(1)}, bf16[2,...) custom-call(f32[4,2,256,128]{3,2,1,0:T(8,128)S(1)} %get-tuple-element.38.refs_0_, ...), custom_call_target="tpu_custom_call" | custom-call | tf_op jit(solution)/shard_map/exchange_first/pallas_call | solution.py:457
  50.3 7.9 %sweep.2 = (f32[4,2,256,128]{3,2,1,0:T(8,128)S(1)}, bf16[4,2,256,128]{3,2,1,0:T(8,128)(2,1)S(1)}) custom-call(s32[2,8]{1,0:T(2,128)S(1)} %bitcast.13, s32[1]{0:T(128)} %bitcast.7.count, bf16[2,2,256,128]{3,2,1,0:T(8,128)(2,1)S(1)} %get-tuple-element.40.own, bf16[2,2,256,128]{3,2,1,0:T(8,128)(2,1)S(1)} %get-tuple-element.41.right, ...), custom_call_target="tpu_custom_call" | custom-call | tf_op jit(solution)/shard_map/sweep/pallas_call | solution.py:446
  58.2 23.4 %exchange.1 = (f32[2,2,256,128]{3,2,1,0:T(8,128)S(1)}, bf16[2,2,256,128]{3,2,1,0:T(8,128)(2,1)S(1)}, bf16[2,2,256,128]{3,2,1,0:T(8,128)(2,1)S(1)}, bf16[2,2,256,...) custom-call(f32[1]{0:T(128)} %bitcast.9.refs_0_, f32[4,2,256,128]{3,2,1,0:T(8,128)S(1)} %get-tuple-element.45.refs_1_, ...), custom_call_target="tpu_custom_call" | custom-call | tf_op jit(solution)/shard_map/exchange/pallas_call | solution.py:467
  81.6 7.9 %sweep.3 = (f32[4,2,256,128]{3,2,1,0:T(8,128)S(1)}, bf16[4,2,256,128]{3,2,1,0:T(8,128)(2,1)S(1)}) custom-call(s32[2,8]{1,0:T(2,128)S(1)} %bitcast.14, s32[1]{0:T(128)} %bitcast.8.count, bf16[2,2,256,128]{3,2,1,0:T(8,128)(2,1)S(1)} %get-tuple-element.48.own, bf16[2,2,256,128]{3,2,1,0:T(8,128)(2,1)S(1)} %get-tuple-element.49.right, ...), custom_call_target="tpu_custom_call" | custom-call | tf_op jit(solution)/shard_map/sweep/pallas_call | solution.py:446
  89.5 24.6 %finish.1 = f32[2,256,256]{2,1,0:T(8,128)S(1)} custom-call(f32[1]{0:T(128)} %bitcast.10.damping, f32[4,2,256,128]{3,2,1,0:T(8,128)S(1)} %get-tuple-element.52.top, bf16[4,2,256,128]{3,2,1,0:T(8,128)(2,1)S(1)} %get-tuple-element.53.bottom, f32[2,2,256,128]{3,2,1,0:T(8,128)S(1)} %get-tuple-element.47.refs_3_.q0_ref, ...), custom_call_target="tpu_custom_call" | custom-call | tf_op jit(solution)/shard_map/finish/pallas_call | solution.py:477
  114.1 0.8 copy.12
Async XLA Ops:
  1.3 1.2 %copy-start = (bf16[1,1,8,256,256]{4,3,2,1,0:T(8,128)(2,1)S(1)}, bf16[1,1,8,256,256]{4,3,2,1,0:T(8,128)(2,1)}, u32[]{:S(2)}) copy-start(bf16[1,1,8,256,256]{4,3,2,1,0:T(8,128)(2,1)} %param.12) | copy-start | bytes 3145732
  2.5 1.0 copy-start.1
  3.6 1.0 copy-start.2
  4.6 1.0 copy-start.3
  5.7 0.9 copy-start.4
  18.5 0.7 copy-start.5

commit v3 on v2

--- a/solution.py
+++ b/solution.py
@@ -196,30 +196,15 @@
             copy.wait_send()
 
 
-def spread_kernel(object_ref, *refs):
-    sources, (own, right, below, corner), targets = refs[:4], refs[4:8], refs[8:12]
-    send_sem, recv_sem, load_sem = refs[12:]
-    loads = [
-        pltpu.make_async_copy(
-            object_ref.at[t, :, pl.ds(h * LANES, LANES)], own.at[h, t], load_sem.at[2 * h + t]
-        )
-        for h in range(2) for t in range(2)
-    ]
-    stages = [
-        pltpu.make_async_copy(source, target, load_sem.at[4 + k])
-        for k, (source, target) in enumerate(zip(sources, targets))
-    ]
-    for copy in loads + stages:
-        copy.start()
+def spread_kernel(object_ref, own, right, below, corner, send_sem, recv_sem):
+    for h in range(2):
+        for t in range(2):
+            own[h, t] = object_ref[t, :, h * LANES:(h + 1) * LANES]
     greet_neighbours()
-    for copy in loads:
-        copy.wait()
     copies = margin_copies(own, right, below, corner, send_sem, recv_sem, 0)
     for c in range(CHUNKS):
         send_margins(copies, c)
     settle_margins(copies)
-    for copy in stages:
-        copy.wait()
 
 
 def exchange_kernel(first, *refs):
@@ -405,7 +390,7 @@
     extent = probe_field.shape[-1]
     tile = object_field.shape[1]
     slots = corners.shape[2]
-    group = 2
+    group = min(4, slots)
     n_y, n_x = lax.axis_size("ty"), lax.axis_size("tx")
     places = corners.reshape(slots, 2).T
     count = counts.reshape(1)
@@ -428,16 +413,16 @@
             collective_id=collective_id, has_side_effects=True, vmem_limit_bytes=16 << 20
         )
 
-    staged = (probe_field, table_f, table_g, measured)
-    *margins, probe_field, table_f, table_g, measured = pl.pallas_call(
+    margins = pl.pallas_call(
         spread_kernel,
-        out_shape=quarters + [shaped(array.shape, array.dtype) for array in staged],
-        in_specs=[pl.BlockSpec(memory_space=pltpu.HBM)] * 5,
-        out_specs=[VMEM_SPEC] * 8,
-        scratch_shapes=sems(3 * CHUNKS) + [pltpu.SemaphoreType.DMA((8,))],
+        out_shape=quarters,
+        in_specs=[VMEM_SPEC],
+        out_specs=[VMEM_SPEC] * 4,
+        scratch_shapes=sems(3 * CHUNKS),
         compiler_params=params(0),
+        cost_estimate=pl.CostEstimate(flops=10**10, bytes_accessed=30 << 20, transcendentals=0),
         name="spread",
-    )(object_field, *staged)
+    )(object_field)
 
     def sweep(margins, extra, first):
         outs = [shaped((4, 2, tile, LANES), F32), shaped((4, 2, tile, LANES), BF16)]

time: 115 us -> 107 us (0.930)
  local copies, waits for them, and re-layouts: 6.76 us -> 1.76 us
  Pallas kernels: 107 us -> 104 us
    unnamed x13, local copies, waits for them, and re-layouts: 6.76 us -> 1.76 us
    pallas_call x1, Pallas kernels: 24.6 us -> 22 us  [per_device(): pl.pallas_call(finish_kernel, out_shape=shaped((2, tile, tile), F32), in_...]
    pallas_call x3, Pallas kernels: 23.7 us -> 25.9 us  [sweep(): pl.pallas_call(functools.partial(sweep_kernel, first, group), out_shape=o...]
    pallas_call x1, Pallas kernels: 23.2 us -> 21.7 us  [per_device(): pl.pallas_call(functools.partial(exchange_kernel, True), out_shape=[shape...]
where the time goes in v3:
time: 107 us
  Pallas kernels  104 us (97%)
  local copies, waits for them, and re-layouts  1.76 us (2%)
  between operations  1.41 us (1%)
    pallas_call x3, Pallas kernels, sweep(): pl.pallas_call(functools.partial(sweep_kernel, first, group), out_shape=o...  25.9 us
    pallas_call x1, Pallas kernels, per_device(): pl.pallas_call(functools.partial(exchange_kernel, False), out_shape=[shap...  22.7 us
    pallas_call x1, Pallas kernels, per_device(): pl.pallas_call(finish_kernel, out_shape=shaped((2, tile, tile), F32), in_...  22 us
    pallas_call x1, Pallas kernels, per_device(): pl.pallas_call(functools.partial(exchange_kernel, True), out_shape=[shape...  21.7 us
    pallas_call x1, Pallas kernels, per_device(): pl.pallas_call(spread_kernel, out_shape=quarters, in_specs=[VMEM_SPEC], o...  11.6 us

profile of v3, /device:TPU:0, one launch (start us, length us, event | category | flops | bytes accessed | tf_op | source)
XLA Modules:
  0.0 107.1 jit_solution(16704296766988727193)
XLA Ops:
  1.3 0.0 copy-start.5
  1.3 0.9 copy-done.5
  2.2 0.0 copy-start
  2.3 0.0 copy-start.1
  2.3 0.0 copy-start.2
  2.3 0.0 copy-start.3
  2.3 0.0 copy-start.4
  2.3 11.6 %spread.1 = (bf16[2,2,256,128]{3,2,1,0:T(8,128)(2,1)S(1)}, bf16[2,2,256,128]{3,2,1,0:T(8,128)(2,1)S(1)}, bf16[2,2,256,128]{3,2,1,0:T(8,128)(2,1)S(1)}, bf16[2,2,256,128]{3,2,1,0:T(8,128)(2,1)S(1)}) custom-call(bf16[2,256,256]{2,1,0:T(8,128)(2,1)S(1)} %copy-done.5), custom_call_target="tpu_custom_call" | custom-call | flops 10000000000 | bytes 31457280 | tf_op jit(solution)/shard_map/spread/pallas_call | solution.py:416
  13.9 0.0 copy-done
  13.9 0.0 copy-done.1
  13.9 0.0 copy-done.2
  13.9 0.0 copy-done.3
  13.9 0.0 copy-done.4
  13.9 8.6 %sweep_first.1 = (f32[4,2,256,128]{3,2,1,0:T(8,128)S(1)}, bf16[4,2,256,128]{3,2,1,0:T(8,128)(2,1)S(1)}, f32[8,2,256,256]{3,2,1,0:T(8,128)S(1)}) custom-call(s32[2,8]{1,0:T(2,128)S(1)} %bitcast.12, s32[1]{0:T(128)} %bitcast.6.count, bf16[2,2,256,128]{3,2,1,0:T(8,128)(2,1)S(1)} %get-tuple-element.26.own, bf16[2,2,256,128]{3,2,1,0:T(8,128)(2,1)S(1)} %get-tuple-element.27.right, ...), custom_call_target="tpu_custom_call" | custom-call | tf_op jit(solution)/shard_map/sweep_first/pallas_call | solution.py:431
  22.6 21.7 %exchange_first.1 = (f32[2,2,256,128]{3,2,1,0:T(8,128)S(1)}, bf16[2,2,256,128]{3,2,1,0:T(8,128)(2,1)S(1)}, bf16[2,2,256,128]{3,2,1,0:T(8,128)(2,1)S(1)}, bf16[2,...) custom-call(f32[4,2,256,128]{3,2,1,0:T(8,128)S(1)} %get-tuple-element.30.refs_0_, ...), custom_call_target="tpu_custom_call" | custom-call | tf_op jit(solution)/shard_map/exchange_first/pallas_call | solution.py:442
  44.3 8.6 %sweep.2 = (f32[4,2,256,128]{3,2,1,0:T(8,128)S(1)}, bf16[4,2,256,128]{3,2,1,0:T(8,128)(2,1)S(1)}) custom-call(s32[2,8]{1,0:T(2,128)S(1)} %bitcast.13, s32[1]{0:T(128)} %bitcast.7.count, bf16[2,2,256,128]{3,2,1,0:T(8,128)(2,1)S(1)} %get-tuple-element.32.own, bf16[2,2,256,128]{3,2,1,0:T(8,128)(2,1)S(1)} %get-tuple-element.33.right, ...), custom_call_target="tpu_custom_call" | custom-call | tf_op jit(solution)/shard_map/sweep/pallas_call | solution.py:431
  52.9 22.7 %exchange.1 = (f32[2,2,256,128]{3,2,1,0:T(8,128)S(1)}, bf16[2,2,256,128]{3,2,1,0:T(8,128)(2,1)S(1)}, bf16[2,2,256,128]{3,2,1,0:T(8,128)(2,1)S(1)}, bf16[2,2,256,...) custom-call(f32[1]{0:T(128)} %bitcast.9.refs_0_, f32[4,2,256,128]{3,2,1,0:T(8,128)S(1)} %get-tuple-element.37.refs_1_, ...), custom_call_target="tpu_custom_call" | custom-call | tf_op jit(solution)/shard_map/exchange/pallas_call | solution.py:452
  75.5 8.7 %sweep.3 = (f32[4,2,256,128]{3,2,1,0:T(8,128)S(1)}, bf16[4,2,256,128]{3,2,1,0:T(8,128)(2,1)S(1)}) custom-call(s32[2,8]{1,0:T(2,128)S(1)} %bitcast.14, s32[1]{0:T(128)} %bitcast.8.count, bf16[2,2,256,128]{3,2,1,0:T(8,128)(2,1)S(1)} %get-tuple-element.40.own, bf16[2,2,256,128]{3,2,1,0:T(8,128)(2,1)S(1)} %get-tuple-element.41.right, ...), custom_call_target="tpu_custom_call" | custom-call | tf_op jit(solution)/shard_map/sweep/pallas_call | solution.py:431
  84.3 22.0 %finish.1 = f32[2,256,256]{2,1,0:T(8,128)S(1)} custom-call(f32[1]{0:T(128)} %bitcast.10.damping, f32[4,2,256,128]{3,2,1,0:T(8,128)S(1)} %get-tuple-element.44.top, bf16[4,2,256,128]{3,2,1,0:T(8,128)(2,1)S(1)} %get-tuple-element.45.bottom, f32[2,2,256,128]{3,2,1,0:T(8,128)S(1)} %get-tuple-element.39.refs_3_.q0_ref, ...), custom_call_target="tpu_custom_call" | custom-call | tf_op jit(solution)/shard_map/finish/pallas_call | solution.py:462
  106.3 0.8 copy.12
Async XLA Ops:
  1.3 1.0 copy-start.5
  2.2 11.6 %copy-start = (f32[2,256,256]{2,1,0:T(8,128)S(1)}, f32[2,256,256]{2,1,0:T(8,128)}, u32[]{:S(2)}) copy-start(f32[2,256,256]{2,1,0:T(8,128)} %probe.5) | copy-start | bytes 1572868
  2.3 11.7 %copy-start.1 = (bf16[512,512]{1,0:T(8,128)(2,1)S(1)}, bf16[512,512]{1,0:T(8,128)(2,1)}, u32[]{:S(2)}) copy-start(bf16[512,512]{1,0:T(8,128)(2,1)} %constant.10.table_g) | copy-start | bytes 1572868
  2.3 11.7 %copy-start.2 = (bf16[512,512]{1,0:T(8,128)(2,1)S(1)}, bf16[512,512]{1,0:T(8,128)(2,1)}, u32[]{:S(2)}) copy-start(bf16[512,512]{1,0:T(8,128)(2,1)} %constant.9.table_f) | copy-start | bytes 1572868
  2.3 11.7 %copy-start.3 = (bf16[1,1,8,256,256]{4,3,2,1,0:T(8,128)(2,1)S(1)}, bf16[1,1,8,256,256]{4,3,2,1,0:T(8,128)(2,1)}, u32[]{:S(2)}) copy-start(bf16[1,1,8,256,256]{4,3,2,1,0:T(8,128)(2,1)} %param.12) | copy-start | bytes 3145732
  2.3 11.7 %copy-start.4 = (s32[1,1,8,2]{2,3,1,0:T(2,128)S(1)}, s32[1,1,8,2]{2,3,1,0:T(2,128)}, u32[]{:S(2)}) copy-start(s32[1,1,8,2]{2,3,1,0:T(2,128)} %param.10) | copy-start | bytes 196

commit v4 on v3

--- a/solution.py
+++ b/solution.py
@@ -290,13 +290,12 @@
 def sweep_kernel(first, group, corners, count, own, right, below, corner, probe, table_f, table_g, extra,
                  top, bottom, *rest):
     if first:
-        psi_ref, field, total = rest
+        psi_ref, turned, field, total = rest
     else:
         field, total = rest
-        psi_ref = extra
-    extent = probe.shape[-1]
+        psi_ref, turned = extra, probe
+    extent = probe.shape[-2]
     tile = own.shape[2]
-    slots = psi_ref.shape[0]
     field[0:2, :, 0:tile] = own[...].astype(F32)
     field[2:4, :, 0:tile] = right[...].astype(F32)
     field[0:2, :, tile:] = below[...].astype(F32)
@@ -305,49 +304,54 @@
     lane = lax.broadcasted_iota(jnp.int32, (extent, LANES), 1)
     live = count[0]
 
+    def turn_probe(s):
+        shift = lax.rem(corners[1, s], LANES)
+        keep = lane >= shift
+        for t in range(2):
+            near = pltpu.roll(probe[t, :, 0:LANES], shift, 1)
+            far = pltpu.roll(probe[t, :, LANES:], shift, 1)
+            turned[s, t, :, 0:LANES] = jnp.where(keep, near, far)
+            turned[s, t, :, LANES:] = jnp.where(keep, far, near)
+
     def cut(s):
         row, col = corners[0, s], corners[1, s]
         block, shift = col // LANES, lax.rem(col, LANES)
-        keep = lane < LANES - shift
-        halves = []
-        for t in range(2):
-            turned = [
-                pltpu.roll(field[block + k, t, pl.ds(row, extent), :], lax.rem(LANES - shift, LANES), 1)
-                for k in range(3)
-            ]
-            halves.append([jnp.where(keep, turned[k], turned[k + 1]) for k in range(2)])
+        keep = lane >= shift
+        rows = pl.ds(row, extent)
         waves = [[], []]
         for k in range(2):
-            probe_re = probe[0, :, k * LANES:(k + 1) * LANES]
-            probe_im = probe[1, :, k * LANES:(k + 1) * LANES]
-            waves[0].append((probe_re * halves[0][k] - probe_im * halves[1][k]).astype(BF16))
-            waves[1].append((probe_re * halves[1][k] + probe_im * halves[0][k]).astype(BF16))
+            halves = []
+            for t in range(2):
+                if k == 0:
+                    halves.append(jnp.where(keep, field[block, t, rows, :], field[block + 2, t, rows, :]))
+                else:
+                    halves.append(field[block + 1, t, rows, :])
+            lanes = slice(k * LANES, (k + 1) * LANES)
+            probe_re, probe_im = turned[s, 0, :, lanes], turned[s, 1, :, lanes]
+            waves[0].append((probe_re * halves[0] - probe_im * halves[1]).astype(BF16))
+            waves[1].append((probe_re * halves[1] + probe_im * halves[0]).astype(BF16))
         return jnp.concatenate(waves[0] + waves[1], 1)
 
     def add(s, back):
         row, col = corners[0, s], corners[1, s]
         block, shift = col // LANES, lax.rem(col, LANES)
         keep = lane >= shift
-        back = back.astype(BF16).astype(F32)
-        for t in range(2):
-            turned = []
-            for k in range(2):
-                lanes = slice(k * LANES, (k + 1) * LANES)
-                probe_re, probe_im = probe[0, :, lanes], probe[1, :, lanes]
-                re, im = back[:extent, lanes], back[extent:, lanes]
+        rows = pl.ds(row, extent)
+        for k in range(2):
+            lanes = slice(k * LANES, (k + 1) * LANES)
+            probe_re, probe_im = turned[s, 0, :, lanes], turned[s, 1, :, lanes]
+            re, im = back[:extent, lanes], back[extent:, lanes]
+            for t in range(2):
                 if t == 0:
                     term = probe_re * re + probe_im * im
                 else:
                     term = probe_re * im - probe_im * re
-                turned.append(pltpu.roll(term, shift, 1))
-            zero = jnp.zeros_like(turned[0])
-            pieces = [
-                jnp.where(keep, turned[0], zero),
-                jnp.where(keep, turned[1], turned[0]),
-                jnp.where(keep, zero, turned[1]),
-            ]
-            for k in range(3):
-                total[block + k, t, pl.ds(row, extent), :] += pieces[k]
+                if k == 0:
+                    zero = jnp.zeros_like(term)
+                    total[block, t, rows, :] += jnp.where(keep, term, zero)
+                    total[block + 2, t, rows, :] += jnp.where(keep, zero, term)
+                else:
+                    total[block + 1, t, rows, :] += term
 
     def transform(waves, rhs, lhs):
         half = jnp.dot(waves, rhs[...], preferred_element_type=F32).astype(BF16)
@@ -359,6 +363,9 @@
 
     def step(index, carry):
         base = index * group
+        if first:
+            for g in range(group):
+                turn_probe(base + g)
         waves = jnp.concatenate([cut(base + g) for g in range(group)], 0)
         image = transform(waves, table_f, table_g)
         mixed = []
@@ -424,10 +431,10 @@
         name="spread",
     )(object_field)
 
-    def sweep(margins, extra, first):
+    def sweep(margins, probe, extra, first):
         outs = [shaped((4, 2, tile, LANES), F32), shaped((4, 2, tile, LANES), BF16)]
         if first:
-            outs.append(shaped((slots, 2, extent, extent), F32))
+            outs += [shaped((slots, 2, extent, extent), F32)] * 2
         return pl.pallas_call(
             functools.partial(sweep_kernel, first, group),
             out_shape=outs,
@@ -436,9 +443,9 @@
             scratch_shapes=[pltpu.VMEM((4, 2, 2 * tile, LANES), F32)] * 2,
             compiler_params=pltpu.CompilerParams(vmem_limit_bytes=36 << 20),
             name="sweep_first" if first else "sweep",
-        )(places, count, *margins, probe_field, table_f, table_g, extra)
-
-    top, bottom, psi = sweep(margins, measured, True)
+        )(places, count, *margins, probe, table_f, table_g, extra)
+
+    top, bottom, psi, turned = sweep(margins, probe_field, measured, True)
     q0, *margins = pl.pallas_call(
         functools.partial(exchange_kernel, True),
         out_shape=[shaped(quarter, F32)] + quarters,
@@ -448,7 +455,7 @@
         compiler_params=params(1),
         name="exchange_first",
     )(top, bottom)
-    top, bottom = sweep(margins, psi, False)
+    top, bottom = sweep(margins, turned, psi, False)
     q1, *margins = pl.pallas_call(
         functools.partial(exchange_kernel, False),
         out_shape=[shaped(quarter, F32)] + quarters,
@@ -458,7 +465,7 @@
         compiler_params=params(2),
         name="exchange",
     )(damping, top, bottom, q0)
-    top, bottom = sweep(margins, psi, False)
+    top, bottom = sweep(margins, turned, psi, False)
     return pl.pallas_call(
         finish_kernel,
         out_shape=shaped((2, tile, tile), F32),

time: 107 us -> 103 us (0.963)
  Pallas kernels: 104 us -> 99.4 us
    pallas_call x1, Pallas kernels: 21.7 us -> 12.7 us  [per_device(): pl.pallas_call(functools.partial(exchange_kernel, True), out_shape=[shape...]
    pallas_call x1, Pallas kernels: 22 us -> 29.7 us  [per_device(): pl.pallas_call(finish_kernel, out_shape=shaped((2, tile, tile), F32), in_...]
    pallas_call x1, Pallas kernels: 22.7 us -> 20.9 us  [per_device(): pl.pallas_call(functools.partial(exchange_kernel, False), out_shape=[shap...]
    pallas_call x3, Pallas kernels: 25.9 us -> 24.5 us  [sweep(): pl.pallas_call(functools.partial(sweep_kernel, first, group), out_shape=o...]
where the time goes in v4:
time: 103 us
  Pallas kernels  99.4 us (97%)
  local copies, waits for them, and re-layouts  1.76 us (2%)
  between operations  1.41 us (1%)
    pallas_call x1, Pallas kernels, per_device(): pl.pallas_call(finish_kernel, out_shape=shaped((2, tile, tile), F32), in_...  29.7 us
    pallas_call x3, Pallas kernels, sweep(): pl.pallas_call(functools.partial(sweep_kernel, first, group), out_shape=o...  24.5 us
    pallas_call x1, Pallas kernels, per_device(): pl.pallas_call(functools.partial(exchange_kernel, False), out_shape=[shap...  20.9 us
    pallas_call x1, Pallas kernels, per_device(): pl.pallas_call(functools.partial(exchange_kernel, True), out_shape=[shape...  12.7 us
    pallas_call x1, Pallas kernels, per_device(): pl.pallas_call(spread_kernel, out_shape=quarters, in_specs=[VMEM_SPEC], o...  11.6 us

profile of v4, /device:TPU:0, one launch (start us, length us, event | category | flops | bytes accessed | tf_op | source)
XLA Modules:
  0.0 102.6 jit_solution(5077256340659137486)
XLA Ops:
  1.3 0.0 copy-start.5
  1.3 0.9 copy-done.5
  2.2 0.0 copy-start
  2.3 0.0 copy-start.1
  2.3 0.0 copy-start.2
  2.3 0.0 copy-start.3
  2.3 0.0 copy-start.4
  2.3 11.6 %spread.1 = (bf16[2,2,256,128]{3,2,1,0:T(8,128)(2,1)S(1)}, bf16[2,2,256,128]{3,2,1,0:T(8,128)(2,1)S(1)}, bf16[2,2,256,128]{3,2,1,0:T(8,128)(2,1)S(1)}, bf16[2,2,256,128]{3,2,1,0:T(8,128)(2,1)S(1)}) custom-call(bf16[2,256,256]{2,1,0:T(8,128)(2,1)S(1)} %copy-done.5), custom_call_target="tpu_custom_call" | custom-call | flops 10000000000 | bytes 31457280 | tf_op jit(solution)/shard_map/spread/pallas_call | solution.py:423
  13.9 0.0 copy-done
  13.9 0.0 copy-done.1
  13.9 0.0 copy-done.2
  13.9 0.0 copy-done.3
  13.9 0.0 copy-done.4
  13.9 8.4 %sweep_first.1 = (f32[4,2,256,128]{3,2,1,0:T(8,128)S(1)}, bf16[4,2,256,128]{3,2,1,0:T(8,128)(2,1)S(1)}, f32[8,2,256,256]{3,2,1,0:T(8,128)S(1)}, f32[8,2,256,256]{3,2,1,0:T(8,128)S(1)}) custom-call(s32[2,8]{1,0:T(2,128)S(1)} %bitcast.12, s32[1]{0:T(128)} %bitcast.6.count, bf16[2,2,256,128]{3,2,1,0:T(8,128)(2,1)S(1)} %get-tuple-element.27.own, ...), custom_call_target="tpu_custom_call" | custom-call | tf_op jit(solution)/shard_map/sweep_first/pallas_call | solution.py:438
  22.4 12.7 %exchange_first.1 = (f32[2,2,256,128]{3,2,1,0:T(8,128)S(1)}, bf16[2,2,256,128]{3,2,1,0:T(8,128)(2,1)S(1)}, bf16[2,2,256,128]{3,2,1,0:T(8,128)(2,1)S(1)}, bf16[2,...) custom-call(f32[4,2,256,128]{3,2,1,0:T(8,128)S(1)} %get-tuple-element.31.refs_0_, ...), custom_call_target="tpu_custom_call" | custom-call | tf_op jit(solution)/shard_map/exchange_first/pallas_call | solution.py:449
  35.1 8.0 %sweep.2 = (f32[4,2,256,128]{3,2,1,0:T(8,128)S(1)}, bf16[4,2,256,128]{3,2,1,0:T(8,128)(2,1)S(1)}) custom-call(s32[2,8]{1,0:T(2,128)S(1)} %bitcast.13, s32[1]{0:T(128)} %bitcast.7.count, bf16[2,2,256,128]{3,2,1,0:T(8,128)(2,1)S(1)} %get-tuple-element.33.own, bf16[2,2,256,128]{3,2,1,0:T(8,128)(2,1)S(1)} %get-tuple-element.34.right, ...), custom_call_target="tpu_custom_call" | custom-call | tf_op jit(solution)/shard_map/sweep/pallas_call | solution.py:438
  43.1 20.9 %exchange.1 = (f32[2,2,256,128]{3,2,1,0:T(8,128)S(1)}, bf16[2,2,256,128]{3,2,1,0:T(8,128)(2,1)S(1)}, bf16[2,2,256,128]{3,2,1,0:T(8,128)(2,1)S(1)}, bf16[2,2,256,...) custom-call(f32[1]{0:T(128)} %bitcast.9.refs_0_, f32[4,2,256,128]{3,2,1,0:T(8,128)S(1)} %get-tuple-element.39.refs_1_, ...), custom_call_target="tpu_custom_call" | custom-call | tf_op jit(solution)/shard_map/exchange/pallas_call | solution.py:459
  64.0 8.0 %sweep.3 = (f32[4,2,256,128]{3,2,1,0:T(8,128)S(1)}, bf16[4,2,256,128]{3,2,1,0:T(8,128)(2,1)S(1)}) custom-call(s32[2,8]{1,0:T(2,128)S(1)} %bitcast.14, s32[1]{0:T(128)} %bitcast.8.count, bf16[2,2,256,128]{3,2,1,0:T(8,128)(2,1)S(1)} %get-tuple-element.42.own, bf16[2,2,256,128]{3,2,1,0:T(8,128)(2,1)S(1)} %get-tuple-element.43.right, ...), custom_call_target="tpu_custom_call" | custom-call | tf_op jit(solution)/shard_map/sweep/pallas_call | solution.py:438
  72.0 29.7 %finish.1 = f32[2,256,256]{2,1,0:T(8,128)S(1)} custom-call(f32[1]{0:T(128)} %bitcast.10.damping, f32[4,2,256,128]{3,2,1,0:T(8,128)S(1)} %get-tuple-element.46.top, bf16[4,2,256,128]{3,2,1,0:T(8,128)(2,1)S(1)} %get-tuple-element.47.bottom, f32[2,2,256,128]{3,2,1,0:T(8,128)S(1)} %get-tuple-element.41.refs_3_.q0_ref, ...), custom_call_target="tpu_custom_call" | custom-call | tf_op jit(solution)/shard_map/finish/pallas_call | solution.py:469
  101.8 0.8 copy.12
Async XLA Ops:
  1.3 1.0 copy-start.5
  2.2 11.6 %copy-start = (bf16[512,512]{1,0:T(8,128)(2,1)S(1)}, bf16[512,512]{1,0:T(8,128)(2,1)}, u32[]{:S(2)}) copy-start(bf16[512,512]{1,0:T(8,128)(2,1)} %constant.10.table_g) | copy-start | bytes 1572868
  2.3 11.7 %copy-start.1 = (bf16[512,512]{1,0:T(8,128)(2,1)S(1)}, bf16[512,512]{1,0:T(8,128)(2,1)}, u32[]{:S(2)}) copy-start(bf16[512,512]{1,0:T(8,128)(2,1)} %constant.9.table_f) | copy-start | bytes 1572868
  2.3 11.7 %copy-start.2 = (bf16[1,1,8,256,256]{4,3,2,1,0:T(8,128)(2,1)S(1)}, bf16[1,1,8,256,256]{4,3,2,1,0:T(8,128)(2,1)}, u32[]{:S(2)}) copy-start(bf16[1,1,8,256,256]{4,3,2,1,0:T(8,128)(2,1)} %param.12) | copy-start | bytes 3145732
  2.3 11.7 %copy-start.3 = (f32[2,256,256]{2,1,0:T(8,128)S(1)}, f32[2,256,256]{2,1,0:T(8,128)}, u32[]{:S(2)}) copy-start(f32[2,256,256]{2,1,0:T(8,128)} %probe.1) | copy-start | bytes 1572868
  2.3 11.7 %copy-start.4 = (s32[1,1,8,2]{2,3,1,0:T(2,128)S(1)}, s32[1,1,8,2]{2,3,1,0:T(2,128)}, u32[]{:S(2)}) copy-start(s32[1,1,8,2]{2,3,1,0:T(2,128)} %param.10) | copy-start | bytes 196

commit v5 on v4

--- a/solution.py
+++ b/solution.py
@@ -64,44 +64,41 @@
     return pl.ds(chunk * size, size)
 
 
-def margin_copies(own, right, below, corner, send_sem, recv_sem, base):
+def margin_copies(out_left, in_right, own, right, below, corner, send_sem, recv_sem, base):
     ty, tx = place()[:2]
     to_left, to_up, on_up = [], [], []
     for c in range(CHUNKS):
         rows = rows_of(c, own.shape[2])
-        part = [ref.at[:, :, rows] for ref in (own, right, below, corner)]
+        part = [ref.at[:, :, rows] for ref in (out_left, in_right, own, right, below, corner)]
         to_left.append(remote(part[0], part[1], send_sem, recv_sem, base + 3 * c, {"tx": tx - 1}))
-        to_up.append(remote(part[0], part[2], send_sem, recv_sem, base + 3 * c + 1, {"ty": ty - 1}))
-        on_up.append(remote(part[1], part[3], send_sem, recv_sem, base + 3 * c + 2, {"ty": ty - 1}))
+        to_up.append(remote(part[2], part[4], send_sem, recv_sem, base + 3 * c + 1, {"ty": ty - 1}))
+        on_up.append(remote(part[3], part[5], send_sem, recv_sem, base + 3 * c + 2, {"ty": ty - 1}))
     return to_left, to_up, on_up
 
 
-def send_margins(copies, c):
+def start_if(present, copy):
+    @pl.when(present)
+    def _():
+        copy.start()
+
+
+def take_right(copies, c, on_arrival):
     ty, tx, has_up, has_down, has_left, has_right = place()
-    to_left, to_up, on_up = copies
-
-    @pl.when(has_left)
-    def _():
-        to_left[c].start()
-
-    @pl.when(has_up)
-    def _():
-        to_up[c].start()
+
+    @pl.when(has_right)
+    def _():
+        copies[0][c].wait_recv()
+        on_arrival()
+
+        @pl.when(has_up)
+        def _():
+            copies[2][c].start()
 
 
 def settle_margins(copies):
     ty, tx, has_up, has_down, has_left, has_right = place()
     to_left, to_up, on_up = copies
 
-    @pl.when(has_right)
-    def _():
-        for c in range(CHUNKS):
-            to_left[c].wait_recv()
-
-            @pl.when(has_up)
-            def _():
-                on_up[c].start()
-
     @pl.when(has_down)
     def _():
         for copy in to_up:
@@ -128,7 +125,8 @@
                 copy.wait_send()
 
 
-def fold_margins(top, bottom, inbox_far, inbox_near, outbox, inbox_side, total, send_sem, recv_sem, use):
+def fold_margins(top, bottom, inbox_far, inbox_near, outbox, inbox_side, total, beside, send_sem, recv_sem,
+                 before_sum, after_sum):
     ty, tx, has_up, has_down, has_left, has_right = place()
     far, near, side, spans = [], [], [], []
     for c in range(CHUNKS):
@@ -146,44 +144,39 @@
 
     @pl.when(has_down)
     def _():
-        for copy in far + near:
-            copy.start()
+        for c in range(CHUNKS):
+            far[c].start()
+            near[c].start()
 
     for c in range(CHUNKS):
+        rows = spans[c]
+
         @pl.when(has_up)
         def _():
             far[c].wait_recv()
-
-            @pl.when(has_right)
-            def _():
-                outbox[:, :, spans[c]] = (
-                    top[2:4, :, spans[c]] + inbox_far[:, :, spans[c]].astype(F32)
-                ).astype(BF16)
-
-        @pl.when(jnp.logical_and(ty == 0, has_right))
-        def _():
-            outbox[:, :, spans[c]] = top[2:4, :, spans[c]].astype(BF16)
+            near[c].wait_recv()
+            beside[:, :, rows] = top[2:4, :, rows] + inbox_far[:, :, rows].astype(F32)
+            total[:, :, rows] = top[0:2, :, rows] + inbox_near[:, :, rows].astype(F32)
+
+        @pl.when(ty == 0)
+        def _():
+            beside[:, :, rows] = top[2:4, :, rows]
+            total[:, :, rows] = top[0:2, :, rows]
 
         @pl.when(has_right)
         def _():
+            outbox[:, :, rows] = beside[:, :, rows].astype(BF16)
             side[c].start()
 
+        before_sum(c, rows)
+
     for c in range(CHUNKS):
-        @pl.when(has_up)
-        def _():
-            near[c].wait_recv()
-            total[:, :, spans[c]] = top[0:2, :, spans[c]] + inbox_near[:, :, spans[c]].astype(F32)
-
-        @pl.when(ty == 0)
-        def _():
-            total[:, :, spans[c]] = top[0:2, :, spans[c]]
-
         @pl.when(has_left)
         def _():
             side[c].wait_recv()
             total[:, :, spans[c]] += inbox_side[:, :, spans[c]].astype(F32)
 
-        use(c, spans[c])
+        after_sum(c, spans[c])
 
     @pl.when(has_down)
     def _():
@@ -201,9 +194,13 @@
         for t in range(2):
             own[h, t] = object_ref[t, :, h * LANES:(h + 1) * LANES]
     greet_neighbours()
-    copies = margin_copies(own, right, below, corner, send_sem, recv_sem, 0)
+    copies = margin_copies(own, right, own, right, below, corner, send_sem, recv_sem, 0)
+    has_up, has_left = place()[2], place()[4]
     for c in range(CHUNKS):
-        send_margins(copies, c)
+        start_if(has_left, copies[0][c])
+        start_if(has_up, copies[1][c])
+    for c in range(CHUNKS):
+        take_right(copies, c, lambda: None)
     settle_margins(copies)
 
 
@@ -212,24 +209,41 @@
         top, bottom = refs[:2]
         refs = refs[2:]
     else:
-        damping, top, bottom, before = refs[:4]
-        refs = refs[4:]
-    q_ref, own, right, below, corner = refs[:5]
-    boxes, (send_sem, recv_sem) = refs[5:10], refs[10:]
-    total = boxes[-1]
+        damping, top, bottom, before, before_right = refs[:5]
+        refs = refs[5:]
+    q_ref, q_right, own, right, below, corner = refs[:6]
+    boxes, (out_left, in_right, send_sem, recv_sem) = refs[6:12], refs[12:]
+    total, beside = boxes[-2:]
+    has_up, has_left = place()[2], place()[4]
     greet_neighbours()
-    copies = margin_copies(own, right, below, corner, send_sem, recv_sem, 3 * CHUNKS)
+    copies = margin_copies(out_left, in_right, own, right, below, corner, send_sem, recv_sem, 3 * CHUNKS)
+
+    def scaled(sums, old, rows):
+        if first:
+            return -2.0 * sums
+        return (4.0 * SCALE) * sums + (damping[0] * SCALE) * old[:, :, rows]
+
+    def send_part(c, rows):
+        @pl.when(has_left)
+        def _():
+            out_left[:, :, rows] = total[:, :, rows].astype(BF16)
+            copies[0][c].start()
 
     def use(c, rows):
-        if first:
-            q = -2.0 * total[:, :, rows]
-        else:
-            q = (4.0 * SCALE) * total[:, :, rows] + (damping[0] * SCALE) * before[:, :, rows]
+        q = scaled(total[:, :, rows], None if first else before, rows)
         q_ref[:, :, rows] = q
         own[:, :, rows] = q.astype(BF16)
-        send_margins(copies, c)
-
-    fold_margins(top, bottom, *boxes, send_sem, recv_sem, use)
+        start_if(has_up, copies[1][c])
+
+        def on_arrival():
+            sums = beside[:, :, rows] + in_right[:, :, rows].astype(F32)
+            q = scaled(sums, None if first else before_right, rows)
+            q_right[:, :, rows] = q
+            right[:, :, rows] = q.astype(BF16)
+
+        take_right(copies, c, on_arrival)
+
+    fold_margins(top, bottom, *boxes, send_sem, recv_sem, send_part, use)
     settle_margins(copies)
 
 
@@ -238,7 +252,7 @@
 
 
 def finish_kernel(damping, top, bottom, q0_ref, q1_ref, out_ref,
-                  inbox_far, inbox_near, outbox, inbox_side, total, sums_y, sums_x,
+                  inbox_far, inbox_near, outbox, inbox_side, total, beside, sums_y, sums_x,
                   send_sem, recv_sem, send_y, recv_y, send_x, recv_x):
     ty, tx, has_up, has_down, has_left, has_right = place()
     n_y, n_x = lax.axis_size("ty"), lax.axis_size("tx")
@@ -249,8 +263,8 @@
                 barrier, inc=1, device_id={axis: lax.rem(me + step, n)}, device_id_type=MESH
             )
     pl.semaphore_wait(barrier, n_y + n_x - 2)
-    fold_margins(top, bottom, inbox_far, inbox_near, outbox, inbox_side, total, send_sem, recv_sem,
-                 lambda c, rows: None)
+    fold_margins(top, bottom, inbox_far, inbox_near, outbox, inbox_side, total, beside, send_sem, recv_sem,
+                 lambda c, rows: None, lambda c, rows: None)
     q0, q1 = q0_ref[...], q1_ref[...]
     q2 = (4.0 * SCALE) * total[...] + (damping[0] * SCALE) * q1
     rows = [lane_sums(q0 * q0), lane_sums(q0 * q1), lane_sums(q1 * q1), lane_sums(q0 * q2), lane_sums(q1 * q2)]
@@ -410,7 +424,7 @@
 
     quarter = (2, 2, tile, LANES)
     quarters = [shaped(quarter, BF16)] * 4
-    boxes = [pltpu.VMEM(quarter, BF16)] * 4 + [pltpu.VMEM(quarter, F32)]
+    boxes = [pltpu.VMEM(quarter, BF16)] * 4 + [pltpu.VMEM(quarter, F32)] * 2
 
     def sems(n):
         return [pltpu.SemaphoreType.DMA((n,)), pltpu.SemaphoreType.DMA((n,))]
@@ -446,25 +460,25 @@
         )(places, count, *margins, probe, table_f, table_g, extra)
 
     top, bottom, psi, turned = sweep(margins, probe_field, measured, True)
-    q0, *margins = pl.pallas_call(
+    q0, q0_right, *margins = pl.pallas_call(
         functools.partial(exchange_kernel, True),
-        out_shape=[shaped(quarter, F32)] + quarters,
+        out_shape=[shaped(quarter, F32)] * 2 + quarters,
         in_specs=[VMEM_SPEC] * 2,
-        out_specs=[VMEM_SPEC] * 5,
-        scratch_shapes=boxes + sems(6 * CHUNKS),
+        out_specs=[VMEM_SPEC] * 6,
+        scratch_shapes=boxes + [pltpu.VMEM(quarter, BF16)] * 2 + sems(6 * CHUNKS),
         compiler_params=params(1),
         name="exchange_first",
     )(top, bottom)
     top, bottom = sweep(margins, turned, psi, False)
-    q1, *margins = pl.pallas_call(
+    q1, _, *margins = pl.pallas_call(
         functools.partial(exchange_kernel, False),
-        out_shape=[shaped(quarter, F32)] + quarters,
-        in_specs=[SMEM_SPEC] + [VMEM_SPEC] * 3,
-        out_specs=[VMEM_SPEC] * 5,
-        scratch_shapes=boxes + sems(6 * CHUNKS),
+        out_shape=[shaped(quarter, F32)] * 2 + quarters,
+        in_specs=[SMEM_SPEC] + [VMEM_SPEC] * 4,
+        out_specs=[VMEM_SPEC] * 6,
+        scratch_shapes=boxes + [pltpu.VMEM(quarter, BF16)] * 2 + sems(6 * CHUNKS),
         compiler_params=params(2),
         name="exchange",
-    )(damping, top, bottom, q0)
+    )(damping, top, bottom, q0, q0_right)
     top, bottom = sweep(margins, turned, psi, False)
     return pl.pallas_call(
         finish_kernel,

time: 103 us -> 102 us (level)
  Pallas kernels: 99.4 us -> 98.2 us
    pallas_call x3, Pallas kernels: 24.5 us -> 2.83 us  [sweep(): pl.pallas_call(functools.partial(sweep_kernel, first, group), out_shape=o...]
    pallas_call x1, Pallas kernels: 12.7 us -> 22.6 us  [per_device(): pl.pallas_call(functools.partial(exchange_kernel, True), out_shape=[shape...]
    pallas_call x1, Pallas kernels: 29.7 us -> 37.2 us  [per_device(): pl.pallas_call(finish_kernel, out_shape=shaped((2, tile, tile), F32), in_...]
    pallas_call x1, Pallas kernels: 20.9 us -> 24.1 us  [per_device(): pl.pallas_call(functools.partial(exchange_kernel, False), out_shape=[shap...]
where the time goes in v5:
time: 102 us; the launch traced here: 101 us
  Pallas kernels  98.2 us (96%)
  local copies, waits for them, and re-layouts  1.76 us (2%)
  between operations  1.41 us (1%)
    pallas_call x1, Pallas kernels, per_device(): pl.pallas_call(finish_kernel, out_shape=shaped((2, tile, tile), F32), in_...  37.2 us
    pallas_call x1, Pallas kernels, per_device(): pl.pallas_call(functools.partial(exchange_kernel, False), out_shape=[shap...  24.1 us
    pallas_call x1, Pallas kernels, per_device(): pl.pallas_call(functools.partial(exchange_kernel, True), out_shape=[shape...  22.6 us
    pallas_call x1, Pallas kernels, per_device(): pl.pallas_call(spread_kernel, out_shape=quarters, in_specs=[VMEM_SPEC], o...  11.6 us
    pallas_call x3, Pallas kernels, sweep(): pl.pallas_call(functools.partial(sweep_kernel, first, group), out_shape=o...  2.83 us

profile of v5, /device:TPU:0, one launch (start us, length us, event | category | flops | bytes accessed | tf_op | source)
XLA Modules:
  0.0 101.4 jit_solution(11127884648342341149)
XLA Ops:
  1.3 0.0 copy-start.5
  1.3 0.9 copy-done.5
  2.2 0.0 copy-start
  2.3 0.0 copy-start.1
  2.3 0.0 copy-start.2
  2.3 0.0 copy-start.3
  2.3 0.0 copy-start.4
  2.3 11.6 %spread.1 = (bf16[2,2,256,128]{3,2,1,0:T(8,128)(2,1)S(1)}, bf16[2,2,256,128]{3,2,1,0:T(8,128)(2,1)S(1)}, bf16[2,2,256,128]{3,2,1,0:T(8,128)(2,1)S(1)}, bf16[2,2,256,128]{3,2,1,0:T(8,128)(2,1)S(1)}) custom-call(bf16[2,256,256]{2,1,0:T(8,128)(2,1)S(1)} %copy-done.5), custom_call_target="tpu_custom_call" | custom-call | flops 10000000000 | bytes 31457280 | tf_op jit(solution)/shard_map/spread/pallas_call | solution.py:437
  13.9 0.0 copy-done
  13.9 0.0 copy-done.1
  13.9 0.0 copy-done.2
  13.9 0.0 copy-done.3
  13.9 0.0 copy-done.4
  13.9 0.9 sweep_first.1
  14.9 22.6 %exchange_first.1 = (f32[2,2,256,128]{3,2,1,0:T(8,128)S(1)}, f32[2,2,256,128]{3,2,1,0:T(8,128)S(1)}, bf16[2,2,256,128]{3,2,1,0:T(8,128)(2,1)S(1)}, bf16[2,2,256,...) custom-call(f32[4,2,256,128]{3,2,1,0:T(8,128)S(1)} %get-tuple-element.32.refs_0_,, ...), custom_call_target="tpu_custom_call" | custom-call | tf_op jit(solution)/shard_map/exchange_first/pallas_call | solution.py:463
  37.5 0.9 sweep.2
  38.4 24.1 %exchange.1 = (f32[2,2,256,128]{3,2,1,0:T(8,128)S(1)}, f32[2,2,256,128]{3,2,1,0:T(8,128)}, bf16[2,2,256,128]{3,2,1,0:T(8,128)(2,1)S(1)}, bf16[2,2,256,128]{3,2,1...) custom-call(f32[1]{0:T(128)} %bitcast.9.refs_0_, ...), custom_call_target="tpu_custom_call" | custom-call | tf_op jit(solution)/shard_map/exchange/pallas_call | solution.py:473
  62.5 0.9 sweep.3
  63.4 37.2 %finish.1 = f32[2,256,256]{2,1,0:T(8,128)S(1)} custom-call(f32[1]{0:T(128)} %bitcast.10.damping, f32[4,2,256,128]{3,2,1,0:T(8,128)S(1)} %get-tuple-element.48.top, bf16[4,2,256,128]{3,2,1,0:T(8,128)(2,1)S(1)} %get-tuple-element.49.bottom, f32[2,2,256,128]{3,2,1,0:T(8,128)S(1)} %get-tuple-element.42.refs_3_.q0_ref, ...), custom_call_target="tpu_custom_call" | custom-call | tf_op jit(solution)/shard_map/finish/pallas_call | solution.py:483
  100.6 0.8 copy.12
Async XLA Ops:
  1.3 1.0 copy-start.5
  2.2 11.6 %copy-start = (bf16[512,512]{1,0:T(8,128)(2,1)S(1)}, bf16[512,512]{1,0:T(8,128)(2,1)}, u32[]{:S(2)}) copy-start(bf16[512,512]{1,0:T(8,128)(2,1)} %constant.10.table_g) | copy-start | bytes 1572868
  2.3 11.7 %copy-start.1 = (bf16[512,512]{1,0:T(8,128)(2,1)S(1)}, bf16[512,512]{1,0:T(8,128)(2,1)}, u32[]{:S(2)}) copy-start(bf16[512,512]{1,0:T(8,128)(2,1)} %constant.9.table_f) | copy-start | bytes 1572868
  2.3 11.7 %copy-start.2 = (bf16[1,1,8,256,256]{4,3,2,1,0:T(8,128)(2,1)S(1)}, bf16[1,1,8,256,256]{4,3,2,1,0:T(8,128)(2,1)}, u32[]{:S(2)}) copy-start(bf16[1,1,8,256,256]{4,3,2,1,0:T(8,128)(2,1)} %param.12) | copy-start | bytes 3145732
  2.3 11.7 %copy-start.3 = (f32[2,256,256]{2,1,0:T(8,128)S(1)}, f32[2,256,256]{2,1,0:T(8,128)}, u32[]{:S(2)}) copy-start(f32[2,256,256]{2,1,0:T(8,128)} %probe.1) | copy-start | bytes 1572868
  2.3 11.7 %copy-start.4 = (s32[1,1,8,2]{2,3,1,0:T(2,128)S(1)}, s32[1,1,8,2]{2,3,1,0:T(2,128)}, u32[]{:S(2)}) copy-start(s32[1,1,8,2]{2,3,1,0:T(2,128)} %param.10) | copy-start | bytes 196
